TPU v7x, 256 devices: a whole 4x4x8 slice. The times are simulated.
256 devices in a mesh: ctx: 32 (over z_hi, x, core), tp: 8 (over y, z_lo).
Axes of the slice: x: 4, y: 4, z: 8 (z_hi: 4, z_lo: 2; z = z_hi * 2 + z_lo), core: 2. Of those that a mesh axis runs over, the one named last changes fastest.
Arguments:
- conv_input: bfloat16 [4096, 10240], P('ctx', 'tp'), may hold values from -6 to 6
- gate_input: bfloat16 [4096, 8192], P('ctx', 'tp'), may hold values from -6 to 6
- dt_raw: float32 [128, 4096], P('tp', 'ctx'), may hold values from -4 to 4
- conv_weight: float32 [4, 10240], P(None, 'tp'), may hold values from -3 to 3
- conv_bias: float32 [10240], P('tp'), may hold values from -3 to 3
- dt_bias: float32 [128], P('tp'), may hold values from -3.5 to -2.5
- a_log: float32 [128], P('tp'), may hold values from -12 to 0, as said below
- norm_gain: float32 [8192], P('tp'), may hold values from 0.5 to 1.5
- reference_out: bfloat16 [4096, 8192], P('ctx', 'tp'), may hold values from -16 to 16
- labels: int32 [64], P('ctx'), may hold values 0 or 1
- doc_lengths: int32 [8], replicated, may hold values from 1 to 2112, 4096 in all
Outputs:
- grad_input: bfloat16 [4096, 10240], P('ctx', 'tp')
- grad_gate: bfloat16 [4096, 8192], P('ctx', 'tp')
- grad_dt: float32 [128, 4096], P('tp', 'ctx')
Inputs may be any that keep to these rules, and one draw needn't show every extreme that they name: `a_log`: one value a head.
All inputs are finite; a program needn't handle non-finite values. No bound on the sum of `labels` on one device may be relied on, other than what follows from the above.
Results may differ from a plain program's by a relative error of at most 0.0015.
Values may be sent and summed in bfloat16 or wider, within the bound.
A program may use at most 128 MiB of HBM per device.

v0:
```python
import jax
import jax.numpy as jnp
from jax import lax
from jax.sharding import Mesh
from jax.sharding import PartitionSpec as P

HEADS = 128
HEAD_DIM = 64
STATE = 128
GROUPS = 8
TAPS = 4
LBLK = 64
D_INNER = 8192
CTX = ("ctx_0", "ctx_1", "ctx_2")


HIGH = lax.Precision.HIGHEST


def from_behind(shard, axis, by):
    length = lax.axis_size(axis)
    pairs = [(i, i + by) for i in range(length) if 0 <= i + by < length]
    return lax.ppermute(shard, axis, pairs)


def nothing_yet(shard, identity):
    return jax.tree.map(
        lambda part, zero: jnp.zeros_like(part) + jnp.asarray(zero, part.dtype), shard, identity
    )


def carried_in(shard, axes, combine, identity, reverse):
    before = start = nothing_yet(shard, identity)
    subtotal = shard
    for axis in reversed(axes):
        length, here = (lax.axis_size(axis), lax.axis_index(axis))
        pieces = jax.tree.map(lambda part: lax.all_gather(part, axis), subtotal)
        inside, subtotal = (start, start)
        for k in reversed(range(length)) if reverse else range(length):
            passed = k > here if reverse else k < here
            subtotal = combine(subtotal, jax.tree.map(lambda part: part[k], pieces))
            inside = jax.tree.map(lambda new, old: jnp.where(passed, new, old), subtotal, inside)
        before = combine(inside, before)
    return before


def sent_to_all(shard, axis):
    copies = jnp.broadcast_to(shard, (lax.axis_size(axis), *shard.shape))
    return lax.all_to_all(copies, axis, split_axis=0, concat_axis=0, tiled=True)


def taken_together(shard, axis):
    everything = sent_to_all(shard, axis)
    return jnp.sum(everything, axis=0)


def doc_index(positions, doc_lengths):
    starts = jnp.cumsum(doc_lengths) - doc_lengths
    return jnp.sum((starts[None, :] <= positions[:, None]).astype(jnp.int32), axis=1) - 1


def silu_parts(value):
    sigma = jax.nn.sigmoid(value)
    return (value * sigma, sigma * (1.0 + value * (1.0 - sigma)))


def compose(earlier, later):
    return (earlier[0] * later[0], later[0][..., None, None] * earlier[1] + later[1])


def on_device(
    conv_input,
    gate_input,
    dt_raw,
    conv_weight,
    conv_bias,
    dt_bias,
    a_log,
    norm_gain,
    reference_out,
    labels,
    doc_lengths,
):
    row_count = conv_input.shape[0]
    channels = conv_input.shape[1]
    head_count = HEADS // GROUPS
    group_width = head_count * HEAD_DIM
    per_group = group_width + 2 * STATE
    groups = channels // per_group
    rim_rows = TAPS - 1
    first_pos = lax.axis_index(CTX) * row_count
    doc_ids = doc_index(first_pos + jnp.arange(row_count, dtype=jnp.int32), doc_lengths)
    prev_doc = doc_index(jnp.reshape(first_pos - 1, (1,)), doc_lengths)[0]
    last_doc = doc_ids[row_count - 1]
    rim_docs = doc_index(
        first_pos - rim_rows + jnp.arange(row_count + rim_rows, dtype=jnp.int32), doc_lengths
    )
    next_docs = doc_index(
        first_pos + jnp.arange(row_count + rim_rows, dtype=jnp.int32), doc_lengths
    )
    incoming = from_behind(conv_input[row_count - rim_rows :], CTX, 1)
    extended = jnp.concatenate([incoming, conv_input], axis=0)
    pre_act = jnp.broadcast_to(conv_bias[None, :], (row_count, channels))
    for tap_index in range(TAPS):
        same_doc = (rim_docs[tap_index : tap_index + row_count] == doc_ids).astype(jnp.float32)[
            :, None
        ]
        pre_act = (
            pre_act
            + conv_weight[tap_index][None, :]
            * extended[tap_index : tap_index + row_count].astype(jnp.float32)
            * same_doc
        )
    activated, slopes = silu_parts(pre_act)
    grouped = activated.reshape(row_count, groups, per_group)
    x_heads = grouped[:, :, :group_width].reshape(row_count, groups, head_count, HEAD_DIM)
    b_rows = grouped[:, :, group_width : group_width + STATE]
    c_rows = grouped[:, :, group_width + STATE :]
    shifted = dt_raw + dt_bias[:, None]
    step_size = jax.nn.softplus(shifted).reshape(groups, head_count, row_count)
    decay_rate = jnp.exp(a_log).reshape(groups, head_count)
    log_cumul = jnp.cumsum(-decay_rate[:, :, None] * step_size, axis=2)
    log_end = log_cumul[:, :, row_count - 1]
    keep_out = (doc_ids == last_doc).astype(jnp.float32)
    keep_in = (doc_ids == prev_doc).astype(jnp.float32)
    lower = jnp.arange(row_count)[:, None] >= jnp.arange(row_count)[None, :]
    allowed = lower & (doc_ids[:, None] == doc_ids[None, :])
    scores = jnp.einsum("tgn,sgn->gts", c_rows, b_rows, precision=HIGH)
    weight_out = jnp.exp(log_end[:, :, None] - log_cumul) * keep_out * step_size
    weight_in = jnp.exp(log_cumul) * keep_in
    passing = jnp.exp(log_end) * (prev_doc == last_doc).astype(jnp.float32)
    pieces = [(0, head_count)]
    start_head, stop_head = pieces[0]
    x_part = x_heads
    weighted = x_part * jnp.transpose(weight_out, (2, 0, 1))[..., None]
    local_state = jnp.einsum("sgn,sgjp->gjnp", b_rows, weighted, precision=HIGH)
    pass_part = passing
    carried = carried_in(
        (pass_part, local_state),
        CTX,
        compose,
        (jnp.ones_like(pass_part), jnp.zeros_like(local_state)),
        False,
    )[1]
    log_gap = (
        log_cumul[:, start_head:stop_head, :, None] - log_cumul[:, start_head:stop_head, None, :]
    )
    decay_mat = jnp.where(allowed, jnp.exp(jnp.where(allowed, log_gap, 0.0)), 0.0)
    mix_mat = scores[:, None] * decay_mat * step_size[:, start_head:stop_head, None, :]
    inner_out = jnp.einsum("gjts,sgjp->tgjp", mix_mat, x_part, precision=HIGH)
    read_out = jnp.einsum("tgn,gjnp->tgjp", c_rows, carried, precision=HIGH)
    w_in = jnp.transpose(weight_in, (2, 0, 1))[..., None]
    outputs = inner_out + read_out * w_in
    stored = [(carried, decay_mat, mix_mat, read_out, weighted)]
    mixer_out = outputs.reshape(row_count, groups, group_width)
    gate_act, gate_slope = silu_parts(
        gate_input.astype(jnp.float32).reshape(row_count, groups, group_width)
    )
    gated_out = mixer_out * gate_act
    inv_rms = lax.rsqrt(jnp.mean(gated_out * gated_out, axis=2, keepdims=True) + 1e-05)
    gain_rows = norm_gain.reshape(groups, group_width)
    normed = gated_out * inv_rms * gain_rows
    target = reference_out.astype(jnp.float32).reshape(row_count, groups, group_width)
    dot_sum, self_sum, ref_sum = (
        taken_together(jnp.sum(normed * target, axis=(1, 2)), "tp"),
        taken_together(jnp.sum(normed * normed, axis=(1, 2)), "tp"),
        taken_together(jnp.sum(target * target, axis=(1, 2)), "tp"),
    )
    mean_dot = dot_sum / D_INNER
    mean_self = self_sum / D_INNER
    mean_ref = ref_sum / D_INNER
    norm_self = jnp.sqrt(mean_self + 1e-06)
    norm_ref = jnp.sqrt(mean_ref + 1e-06)
    cosine = mean_dot / (norm_self * norm_ref)
    distance = jnp.sqrt(mean_self - 2.0 * mean_dot + mean_ref + 1e-06)
    harmful = jnp.repeat(labels, LBLK).astype(jnp.float32)
    coef_self = -harmful * cosine / (norm_self * norm_self) + (1.0 - harmful) / distance
    coef_ref = harmful / (norm_self * norm_ref) - (1.0 - harmful) / distance
    grad_normed = coef_self[:, None, None] * normed + coef_ref[:, None, None] * target
    scaled = grad_normed * gain_rows
    grad_gated = inv_rms * scaled - gated_out * inv_rms * inv_rms * inv_rms * jnp.mean(
        scaled * gated_out, axis=2, keepdims=True
    )
    grad_gate = (
        (grad_gated * mixer_out * gate_slope)
        .reshape(row_count, groups * group_width)
        .astype(jnp.bfloat16)
    )
    grad_mixer = (grad_gated * gate_act).reshape(row_count, groups, head_count, HEAD_DIM)
    grad_scores = jnp.zeros((groups, row_count, row_count), jnp.float32)
    grad_b = jnp.zeros_like(b_rows)
    grad_c = jnp.zeros_like(c_rows)
    grad_x_parts = []
    grad_step_parts = []
    grad_cum_parts = []
    for (start_head, stop_head), saved_item in zip(pieces, stored):
        carried, decay_mat, mix_mat, read_out, weighted = saved_item
        x_part = x_heads
        w_in = jnp.transpose(weight_in, (2, 0, 1))[..., None]
        grad_in = grad_mixer * w_in
        own_term = jnp.einsum("tgn,tgjp->gjnp", c_rows, grad_in, precision=HIGH)
        pass_part = passing
        adjoint = carried_in(
            (pass_part, own_term),
            CTX,
            compose,
            (jnp.ones_like(pass_part), jnp.zeros_like(own_term)),
            True,
        )[1]
        grad_c = grad_c + jnp.einsum("tgjp,gjnp->tgn", grad_in, carried, precision=HIGH)
        grad_cum = jnp.transpose(jnp.sum(read_out * grad_mixer, axis=3), (1, 2, 0)) * weight_in
        from_later = jnp.einsum("sgn,gjnp->sgjp", b_rows, adjoint, precision=HIGH)
        grad_x = from_later * jnp.transpose(weight_out, (2, 0, 1))[..., None]
        grad_weight = jnp.transpose(jnp.sum(from_later * x_part, axis=3), (1, 2, 0))
        grad_b = grad_b + jnp.einsum("sgjp,gjnp->sgn", weighted, adjoint, precision=HIGH)
        out_flow = grad_weight * weight_out
        grad_end = jnp.sum(out_flow, axis=2) + jnp.sum(carried * adjoint, axis=(2, 3)) * pass_part
        grad_cum = grad_cum - out_flow
        grad_step = (
            grad_weight * jnp.exp(log_end[:, start_head:stop_head, None] - log_cumul) * keep_out
        )
        grad_mix = jnp.einsum("tgjp,sgjp->gjts", grad_mixer, x_part, precision=HIGH)
        grad_x = grad_x + jnp.einsum("gjts,tgjp->sgjp", mix_mat, grad_mixer, precision=HIGH)
        weighted_grad = grad_mix * mix_mat
        grad_cum = grad_cum + jnp.sum(weighted_grad, axis=3) - jnp.sum(weighted_grad, axis=2)
        via_mask = grad_mix * decay_mat
        grad_scores = grad_scores + jnp.sum(
            via_mask * step_size[:, start_head:stop_head, None, :], axis=1
        )
        grad_step = grad_step + jnp.sum(via_mask * scores[:, None], axis=2)
        grad_cum = grad_cum.at[:, :, row_count - 1].add(grad_end)
        grad_x_parts.append(grad_x)
        grad_step_parts.append(grad_step)
        grad_cum_parts.append(grad_cum)
    grad_xs = grad_x_parts[0]
    grad_steps = grad_step_parts[0]
    grad_cums = grad_cum_parts[0]
    grad_c = grad_c + jnp.einsum("gts,sgn->tgn", grad_scores, b_rows, precision=HIGH)
    grad_b = grad_b + jnp.einsum("gts,tgn->sgn", grad_scores, c_rows, precision=HIGH)
    grad_log = jnp.flip(jnp.cumsum(jnp.flip(grad_cums, 2), axis=2), 2)
    grad_steps = grad_steps - decay_rate[:, :, None] * grad_log
    grad_dt = grad_steps.reshape(groups * head_count, row_count) * jax.nn.sigmoid(shifted)
    grad_act = jnp.concatenate(
        [grad_xs.reshape(row_count, groups, group_width), grad_b, grad_c], axis=2
    ).reshape(row_count, channels)
    grad_pre = grad_act * slopes
    following = from_behind(grad_pre[:rim_rows], CTX, -1)
    spread = jnp.concatenate([grad_pre, following], axis=0)
    input_grad = jnp.zeros((row_count, channels), jnp.float32)
    for tap_index in range(TAPS):
        offset = rim_rows - tap_index
        same_doc = (next_docs[offset : offset + row_count] == doc_ids).astype(jnp.float32)[:, None]
        input_grad = (
            input_grad
            + conv_weight[tap_index][None, :] * spread[offset : offset + row_count] * same_doc
        )
    return (input_grad.astype(jnp.bfloat16), grad_gate, grad_dt)


def solution(mesh):
    finer = Mesh(mesh.devices.reshape(4, 4, 2, mesh.shape["tp"]), ("ctx_0", "ctx_1", "ctx_2", "tp"))
    in_specs = (
        P(CTX, "tp"),
        P(CTX, "tp"),
        P("tp", CTX),
        P(None, "tp"),
        P("tp"),
        P("tp"),
        P("tp"),
        P("tp"),
        P(CTX, "tp"),
        P(CTX),
        P(),
    )
    out_specs = (P(CTX, "tp"), P(CTX, "tp"), P("tp", CTX))
    return jax.shard_map(
        on_device, mesh=finer, in_specs=in_specs, out_specs=out_specs, check_vma=False
    )
```

profile of v0, /device:TPU:1, one launch (start us, length us, event | category | flops | bytes accessed | tf_op | source)
XLA Modules:
  0.0 324.4 jit_solution(3329446616735397040)
XLA Ops:
  8.0 4.5 %collective-permute-start = (bf16[3,1280]{1,0:T(4,128)(2,1)S(1)}, bf16[3,1280]{1,0:T(4,128)(2,1)S(1)}, u32[]{:S(2)}, u32[]{:S(2)}) collective-permute-start(bf16[3,1280]{1,0:T(4,128)(2,1)S(1)} %slice.222), channel_id=1, source_target_pairs={{0,8},{8,16},{16,24},{24,32},{32,40},{40,48},{48,56},{56,64},{64,7... | collective-permute-start | bytes 23048 | tf_op jit(solution)/shard_map/ppermute | solution.py:23
  12.5 0.8 reduce-window.9
  13.4 1.3 fusion.95
  16.7 1.2 fusion.104
  19.9 1.3 compare_convert_fusion.3
  21.9 0.9 slice_reduce_fusion.3
  23.2 1.7 multiply_bitcast_fusion
  24.9 1.0 slice_multiply_fusion.3
  26.2 1.4 convolution_bitcast_fusion.4
  27.6 1.8 all-gather
  30.0 9.4 %all-gather.3 = f32[4,16,1]{1,2,0:T(1,128)S(1)} all-gather(f32[1,16,1]{1,2,0:T(1,128)S(1)} %get-tuple-element.99), channel_id=5, replica_groups=mesh['ctx_0'=4,'ctx_1'=4,'ctx_2'=2,'tp'=8] {'ctx_1'}, dimensions={0}, use_global_device_ids=true | all-gather | bytes 320 | tf_op jit(solution)/shard_map/all_gather | solution.py:37
  39.9 5.0 %all-gather.19.cloned.1.call-done = f32[2,16,128,64]{2,3,1,0:T(8,128)} async-done(((f32[1,16,128,64]{2,3,1,0:T(8,128)}), f32[2,16,128,64]{2,3,1,0:T(8,128)}) %all-gather.19.cloned.1.call-update) | async-done | bytes 1048592 | tf_op jit(solution)/shard_map/all_gather | solution.py:37
  45.0 2.1 bitcast_add_fusion.18
  47.7 33.3 %all-gather.11.cloned.1.call-done = f32[4,1,16,128,64]{3,4,2,1,0:T(8,128)} async-done(((f32[1,1,16,128,64]{3,4,2,1,0:T(8,128)}), f32[4,1,16,128,64]{3,4,2,1,0:T(8,128)}) %all-gather.11.cloned.1.call-update) | async-done | bytes 2097168 | tf_op jit(solution)/shard_map/all_gather | solution.py:37
  81.0 2.5 multiply_add_fusion.4
  85.8 1.1 copy.142
  87.0 1.8 copy.141
  88.8 1.2 bitcast_multiply_fusion.8
  89.9 10.0 %all_gather.51 = f32[4,1,16]{2,1,0:T(1,128)S(1)} all-gather(f32[1,1,16]{2,1,0:T(1,128)S(1)} %get-tuple-element.76), channel_id=1, replica_groups=mesh['ctx_0'=4,'ctx_1'=4,'ctx_2'=2,'tp'=8] {'ctx_0'}, dimensions={0}, use_global_device_ids=true | all-gather | bytes 320 | tf_op jit(solution)/shard_map/all_gather | solution.py:37
  99.9 1.3 fusion.94
  101.8 1.4 fusion.83
  103.2 2.0 copy.131
  105.3 1.8 fusion.79
  107.0 27.5 %all-gather.13.cloned.1.call-done = f32[4,1,16,128,64]{3,4,2,1,0:T(8,128)} async-done(((f32[1,1,16,128,64]{3,4,2,1,0:T(8,128)}), f32[4,1,16,128,64]{3,4,2,1,0:T(8,128)}) %all-gather.13.cloned.1.call-update) | async-done | bytes 2097168 | tf_op jit(solution)/shard_map/all_gather | solution.py:37
  134.5 2.9 add_add_fusion.1
  137.5 1.5 convolution_bitcast_fusion.3
  139.1 2.2 fusion.1
  142.7 11.0 %all_to_all.18 = f32[8,1,128]{2,1,0:T(1,128)} all-to-all(f32[8,1,128]{2,1,0:T(1,128)S(1)} %broadcast_in_dim.24), channel_id=1, replica_groups=mesh['ctx_0'=4,'ctx_1'=4,'ctx_2'=2,'tp'=8] {'tp'}, dimensions={0} | all-to-all | bytes 8192 | tf_op jit(solution)/shard_map/all_to_all | solution.py:49
  153.7 7.9 %all_to_all.19 = f32[8,1,128]{2,1,0:T(1,128)} all-to-all(f32[8,1,128]{2,1,0:T(1,128)S(1)} %broadcast_in_dim.22), channel_id=1, replica_groups=mesh['ctx_0'=4,'ctx_1'=4,'ctx_2'=2,'tp'=8] {'tp'}, dimensions={0} | all-to-all | bytes 8192 | tf_op jit(solution)/shard_map/all_to_all | solution.py:49
  162.1 3.8 %all-to-all-start.1 = ((f32[8,1,128]{2,1,0:T(1,128)}), f32[8,1,128]{2,1,0:T(1,128)}, u32[]{:S(2)}, u32[]{:S(2)}) async-start(f32[8,1,128]{2,1,0:T(1,128)} %broadcast_in_dim.23), calls=%async_computation.1 | async-start | bytes 8192 | tf_op jit(solution)/shard_map/all_to_all | solution.py:49
  167.4 1.3 convert_element_type.108
  168.7 1.2 reduce_sum.203
  170.0 1.2 reduce_sum.199
  171.2 1.2 reduce_sum.201
  173.8 1.3 multiply_reduce_fusion.4
  175.1 2.7 bitcast_multiply_fusion
  178.6 2.2 convolution_bitcast_fusion.2
  180.9 16.1 %all-gather.21.cloned.1.call-done = f32[2,16,128,64]{2,3,1,0:T(8,128)} async-done(((f32[1,16,128,64]{2,3,1,0:T(8,128)}), f32[2,16,128,64]{2,3,1,0:T(8,128)}) %all-gather.21.cloned.1.call-update) | async-done | bytes 1048592 | tf_op jit(solution)/shard_map/all_gather | solution.py:37
  197.0 2.2 bitcast_add_fusion.16
  199.2 33.8 %all-gather.15.cloned.1.call-done = f32[4,1,16,128,64]{3,4,2,1,0:T(8,128)} async-done(((f32[1,1,16,128,64]{3,4,2,1,0:T(8,128)}), f32[4,1,16,128,64]{3,4,2,1,0:T(8,128)}) %all-gather.15.cloned.1.call-update) | async-done | bytes 2097168 | tf_op jit(solution)/shard_map/all_gather | solution.py:37
  233.1 2.5 multiply_add_fusion.1
  236.4 10.1 %all_gather.50 = f32[4,1,16]{2,1,0:T(1,128)S(1)} all-gather(f32[1,1,16]{2,1,0:T(1,128)S(1)} %copy-done.67), channel_id=1, replica_groups=mesh['ctx_0'=4,'ctx_1'=4,'ctx_2'=2,'tp'=8] {'ctx_0'}, dimensions={0}, use_global_device_ids=true | all-gather | bytes 320 | tf_op jit(solution)/shard_map/all_gather | solution.py:37
  247.1 1.3 multiply_reduce_fusion.2
  249.1 4.4 %fusion.20 = (f32[16,128]{1,0:T(8,128)}, f32[16,128]{1,0:T(8,128)}, f32[16,128]{1,0:T(8,128)}, f32[128,128]{1,0:T(8,128)}) fusion(f32[16,128]{1,0:T(8,128)} %copy.135, f32[16,128]{1,0:T(8,128)} %bitcast.396, f32[128,128]{1,0:T(8,128)} %fusion.79, pred[128,128]{1,0:T(8,128)(4,1)} %fusion.83, f32[128,16,64]{0,2,1:T(8,128)} %bitcast.391, ...), kind=kOutput, calls=%fused_computation.49 | convolution fusion | flops 204711936 | bytes 1236992 | tf_op jit(solution)/shard_map/tgjp,sgjp->gjts/dot_general | solution.py:222
  253.5 1.4 copy.159
  254.9 1.4 copy.160
  256.3 1.4 copy.157
  257.8 0.8 copy.163
  258.6 2.2 convolution_bitcast_fusion.6
  260.8 1.1 fusion.2
  261.9 24.6 %all-gather.17.cloned.1.call-done = f32[4,1,16,128,64]{3,4,2,1,0:T(8,128)} async-done(((f32[1,1,16,128,64]{3,4,2,1,0:T(8,128)}), f32[4,1,16,128,64]{3,4,2,1,0:T(8,128)}) %all-gather.17.cloned.1.call-update) | async-done | bytes 2097168 | tf_op jit(solution)/shard_map/all_gather | solution.py:37
  286.5 3.9 %add_add_fusion = f32[1,1,16,128,64]{3,4,2,1,0:T(8,128)S(1)} fusion(f32[4,1,16,128,64]{3,4,2,1,0:T(8,128)} %all-gather.17.cloned.1.call-done, f32[4,1,16,128,64]{3,4,2,1,0:T(8,128)} %all-gather.15.cloned.1.call-done, f32[2,16,128,64]{2,3,1,0:T(8,128)} %all-gather.21.cloned.1.call-done, f32[16]{0:T(128)} %get-tuple-element.47, f32[16]{0:T(128)} %get-tuple-element.96, ...), kind=kLoop, calls=%fused_computation.104 | loop fusion | flops 4063232 | bytes 5767946 | tf_op jit(solution)/shard_map/add | solution.py:68
  290.5 1.0 convolution_bitcast_fusion.7
  291.6 2.0 multiply_reduce_fusion.3
  293.6 1.1 fusion.3
  294.8 2.2 fusion
  297.0 2.1 copy.152
  299.1 1.5 fusion.18
  300.6 0.9 copy-done.8
  302.1 3.8 %collective-permute-start.1 = (f32[3,1280]{1,0:T(4,128)}, f32[3,1280]{1,0:T(4,128)}, u32[]{:S(2)}, u32[]{:S(2)}) collective-permute-start(f32[3,1280]{1,0:T(4,128)} %slice.321), channel_id=1, source_target_pairs={{8,0},{16,8},{24,16},{32,24},{40,32},{48,40},{56,48},{64,56},{72,6... | collective-permute-start | bytes 46088 | tf_op jit(solution)/shard_map/ppermute | solution.py:23
  305.9 0.8 copy.154
  306.7 0.9 fusion.92
  307.8 4.3 %fusion.37 = f32[16]{0:T(128)S(1)} fusion(f32[4,1,16,128,64]{3,4,2,1,0:T(8,128)} %all-gather.17.cloned.1.call-done, f32[4,1,16,128,64]{3,4,2,1,0:T(8,128)} %all-gather.15.cloned.1.call-done, f32[2,16,128,64]{2,3,1,0:T(8,128)} %all-gather.21.cloned.1.call-done, f32[4,1,16,128,64]{3,4,2,1,0:T(8,128)} %all-gather.13.cloned.1.call-done, ...), kind=kLoop, calls=%fused_computation.67 | loop fusion | flops 8388592 | bytes 10487252 | tf_op jit(solution)/shard_map/reduce_sum | solution.py:217
  314.1 3.4 %fusion.12 = bf16[128,1280]{1,0:T(8,128)(2,1)} fusion(f32[128,1280]{1,0:T(8,128)} %copy-done.8, f32[3,1280]{1,0:T(4,128)} %collective-permute-done.1, f32[128]{0:T(128)S(1)} %copy-done.61, f32[128]{0:T(128)S(1)} %copy-done.62, f32[128]{0:T(128)S(1)} %copy-done.63, f32[128]{0:T(128)S(1)} %copy-done.60, f32[1280]{0:T(1024)S(1)} %copy-done.25, ...), kind=kLoop, calls=%fused_computation.36 | loop fusion | flops 2457600 | bytes 1020928 | tf_op jit(solution)/shard_map/convert_element_type | solution.py:257
  (203 shorter events, 19.5 us)
Async XLA Ops:
  7.2 16.0 %copy-start.18 = (bf16[128,1280]{1,0:T(8,128)(2,1)S(1)}, bf16[128,1280]{1,0:T(8,128)(2,1)}, u32[]{:S(2)}) copy-start(bf16[128,1280]{1,0:T(8,128)(2,1)} %param.13) | copy-start | bytes 983044
  7.2 16.0 %copy-start.46 = (f32[1280]{0:T(1024)S(1)}, f32[1280]{0:T(1024)}, u32[]{:S(2)}) copy-start(f32[1280]{0:T(1024)} %param.17) | copy-start | bytes 15364
  7.2 37.8 %all-gather.19.cloned.1.call-start = ((), (), s32[]{:S(2)}) async-start(), calls=%async_computation.7 | async-start | bytes 1572864 | tf_op jit(solution)/shard_map/all_gather | solution.py:37
  8.0 15.2 %collective-permute-start = (bf16[3,1280]{1,0:T(4,128)(2,1)S(1)}, bf16[3,1280]{1,0:T(4,128)(2,1)S(1)}, u32[]{:S(2)}, u32[]{:S(2)}) collective-permute-start(bf16[3,1280]{1,0:T(4,128)(2,1)S(1)} %slice.222), channel_id=1, source_target_pairs={{0,8},{8,16},{16,24},{24,32},{32,40},{40,48},{48,56},{56,64},{64,7... | collective-permute-start | bytes 23048 | tf_op jit(solution)/shard_map/ppermute | solution.py:23
  18.6 4.2 %copy-start.16 = (f32[16,128]{0,1:T(8,128)}, f32[16,128]{0,1:T(8,128)S(1)}, u32[]{:S(2)}) copy-start(f32[16,128]{0,1:T(8,128)S(1)} %copy.128) | copy-start | bytes 24580
  19.7 64.6 %copy-start.28 = (f32[1,16,128]{2,1,0:T(8,128)}, f32[1,16,128]{2,1,0:T(8,128)S(1)}, u32[]{:S(2)}) copy-start(f32[1,16,128]{2,1,0:T(8,128)S(1)} %reduce_window_sum.27) | copy-start | bytes 24580
  21.3 63.8 %copy-start.58 = (f32[128]{0:T(128)}, f32[128]{0:T(128)S(1)}, u32[]{:S(2)}) copy-start(f32[128]{0:T(128)S(1)} %get-tuple-element.107) | copy-start | bytes 1540
  21.3 6.4 %copy-start.65 = (f32[1,16,1]{1,2,0:T(1,128)}, f32[1,16,1]{1,2,0:T(1,128)S(1)}, u32[]{:S(2)}) copy-start(f32[1,16,1]{1,2,0:T(1,128)S(1)} %get-tuple-element.67) | copy-start | bytes 196
  26.2 54.8 %copy-start.5 = (f32[128,1,1024]{0,2,1:T(8,128)}, f32[128,1,1024]{0,2,1:T(8,128)S(1)}, u32[]{:S(2)}) copy-start(f32[128,1,1024]{0,2,1:T(8,128)S(1)} %copy.138) | copy-start | bytes 1572868
  27.6 53.4 %all-gather.11.cloned.1.call-start = ((), (), s32[]{:S(2)}) async-start(), calls=%async_computation.3 | async-start | bytes 2621440 | tf_op jit(solution)/shard_map/all_gather | solution.py:37
  29.4 17.7 %copy-start.45 = (f32[2,16,1]{1,2,0:T(1,128)}, f32[2,16,1]{1,2,0:T(1,128)S(1)}, u32[]{:S(2)}) copy-start(f32[2,16,1]{1,2,0:T(1,128)S(1)} %all-gather) | copy-start | bytes 388
  30.0 17.2 %copy-start.49 = (f32[16]{0:T(128)}, f32[16]{0:T(128)S(1)}, u32[]{:S(2)}) copy-start(f32[16]{0:T(128)S(1)} %get-tuple-element.98) | copy-start | bytes 196
  39.4 44.2 %copy-start.33 = (f32[4,16,1]{1,2,0:T(1,128)}, f32[4,16,1]{1,2,0:T(1,128)S(1)}, u32[]{:S(2)}) copy-start(f32[4,16,1]{1,2,0:T(1,128)S(1)} %all-gather.3) | copy-start | bytes 772
  39.9 43.6 %copy-start.50 = (f32[16]{0:T(128)}, f32[16]{0:T(128)S(1)}, u32[]{:S(2)}) copy-start(f32[16]{0:T(128)S(1)} %get-tuple-element.77) | copy-start | bytes 196
  39.9 43.6 %copy-start.52 = (f32[16]{0:T(128)}, f32[16]{0:T(128)S(1)}, u32[]{:S(2)}) copy-start(f32[16]{0:T(128)S(1)} %get-tuple-element.95) | copy-start | bytes 196
  47.2 87.3 %all-gather.13.cloned.1.call-start = ((), (), s32[]{:S(2)}) async-start(), calls=%async_computation.4 | async-start | bytes 2621440 | tf_op jit(solution)/shard_map/all_gather | solution.py:37
  47.7 37.2 %copy-start.39 = (f32[16]{0:T(128)}, f32[16]{0:T(128)S(1)}, u32[]{:S(2)}) copy-start(f32[16]{0:T(128)S(1)} %get-tuple-element.80) | copy-start | bytes 196
  47.7 37.2 %copy-start.41 = (f32[16]{0:T(128)}, f32[16]{0:T(128)S(1)}, u32[]{:S(2)}) copy-start(f32[16]{0:T(128)S(1)} %get-tuple-element.81) | copy-start | bytes 196
  47.7 37.2 %copy-start.54 = (f32[16]{0:T(128)}, f32[16]{0:T(128)S(1)}, u32[]{:S(2)}) copy-start(f32[16]{0:T(128)S(1)} %get-tuple-element.82) | copy-start | bytes 196
  83.6 50.9 %copy-start = (f32[4,1,16,128,64]{3,4,2,1,0:T(8,128)S(1)}, f32[4,1,16,128,64]{3,4,2,1,0:T(8,128)}, u32[]{:S(2)}) copy-start(f32[4,1,16,128,64]{3,4,2,1,0:T(8,128)} %all-gather.11.cloned.1.call-done) | copy-start | bytes 6291460
  83.6 50.9 %copy-start.1 = (f32[2,16,128,64]{2,3,1,0:T(8,128)S(1)}, f32[2,16,128,64]{2,3,1,0:T(8,128)}, u32[]{:S(2)}) copy-start(f32[2,16,128,64]{2,3,1,0:T(8,128)} %all-gather.19.cloned.1.call-done) | copy-start | bytes 3145732
  134.5 4.6 %copy-start.11 = (f32[128,1,1024]{0,2,1:T(8,128)S(1)}, f32[128,1,1024]{0,2,1:T(8,128)}, u32[]{:S(2)}) copy-start(f32[128,1,1024]{0,2,1:T(8,128)} %copy.131) | copy-start | bytes 1572868
  134.5 4.6 %copy-start.29 = (f32[1,16,128]{2,1,0:T(8,128)S(1)}, f32[1,16,128]{2,1,0:T(8,128)}, u32[]{:S(2)}) copy-start(f32[1,16,128]{2,1,0:T(8,128)} %copy-done.28) | copy-start | bytes 24580
  134.5 4.6 %copy-start.31 = (f32[128,128]{1,0:T(8,128)S(1)}, f32[128,128]{1,0:T(8,128)}, u32[]{:S(2)}) copy-start(f32[128,128]{1,0:T(8,128)} %fusion.79) | copy-start | bytes 196612
  134.5 4.6 %copy-start.37 = (f32[128,16]{0,1:T(8,128)S(1)}, f32[128,16]{0,1:T(8,128)}, u32[]{:S(2)}) copy-start(f32[128,16]{0,1:T(8,128)} %copy.140) | copy-start | bytes 24580
  134.5 4.6 %copy-start.43 = (pred[128,128]{1,0:T(8,128)(4,1)S(1)}, pred[128,128]{1,0:T(8,128)(4,1)}, u32[]{:S(2)}) copy-start(pred[128,128]{1,0:T(8,128)(4,1)} %fusion.83) | copy-start | bytes 49156
  134.5 4.6 %copy-start.47 = (f32[16,128]{1,0:T(8,128)S(1)}, f32[16,128]{1,0:T(8,128)}, u32[]{:S(2)}) copy-start(f32[16,128]{1,0:T(8,128)} %copy.135) | copy-start | bytes 24580
  137.5 4.1 %copy-start.3 = (f32[1,1,16,128,64]{3,4,2,1,0:T(8,128)}, f32[1,1,16,128,64]{3,4,2,1,0:T(8,128)S(1)}, u32[]{:S(2)}) copy-start(f32[1,1,16,128,64]{3,4,2,1,0:T(8,128)S(1)} %add_add_fusion.1) | copy-start | bytes 1572868
  137.5 3.9 %copy-start.9 = (bf16[128,1024]{0,1:T(8,128)(2,1)S(1)}, bf16[128,1024]{0,1:T(8,128)(2,1)}, u32[]{:S(2)}) copy-start(bf16[128,1024]{0,1:T(8,128)(2,1)} %copy.141) | copy-start | bytes 786436
  141.6 19.9 %copy-start.55 = (f32[128]{0:T(128)}, f32[128]{0:T(128)S(1)}, u32[]{:S(2)}) copy-start(f32[128]{0:T(128)S(1)} %add_rsqrt_fusion) | copy-start | bytes 1540
  162.1 9.0 %all-to-all-start.1 = ((f32[8,1,128]{2,1,0:T(1,128)}), f32[8,1,128]{2,1,0:T(1,128)}, u32[]{:S(2)}, u32[]{:S(2)}) async-start(f32[8,1,128]{2,1,0:T(1,128)} %broadcast_in_dim.23), calls=%async_computation.1 | async-start | bytes 8192 | tf_op jit(solution)/shard_map/all_to_all | solution.py:49
  166.0 31.0 %all-gather.21.cloned.1.call-start = ((), (), s32[]{:S(2)}) async-start(), calls=%async_computation.8 | async-start | bytes 1572864 | tf_op jit(solution)/shard_map/all_gather | solution.py:37
  177.8 55.2 %copy-start.40 = (f32[16]{0:T(128)S(1)}, f32[16]{0:T(128)}, u32[]{:S(2)}) copy-start(f32[16]{0:T(128)} %copy-done.39) | copy-start | bytes 196
  177.8 55.2 %copy-start.42 = (f32[16]{0:T(128)S(1)}, f32[16]{0:T(128)}, u32[]{:S(2)}) copy-start(f32[16]{0:T(128)} %copy-done.41) | copy-start | bytes 196
  177.8 55.2 %copy-start.51 = (f32[16]{0:T(128)S(1)}, f32[16]{0:T(128)}, u32[]{:S(2)}) copy-start(f32[16]{0:T(128)} %get-tuple-element.78) | copy-start | bytes 196
  177.8 55.2 %copy-start.53 = (f32[16]{0:T(128)S(1)}, f32[16]{0:T(128)}, u32[]{:S(2)}) copy-start(f32[16]{0:T(128)} %get-tuple-element.79) | copy-start | bytes 196
  180.8 52.2 %all-gather.15.cloned.1.call-start = ((), (), s32[]{:S(2)}) async-start(), calls=%async_computation.5 | async-start | bytes 2621440 | tf_op jit(solution)/shard_map/all_gather | solution.py:37
  199.2 36.5 %copy-start.38 = (f32[1,16,128]{2,1,0:T(8,128)S(1)}, f32[1,16,128]{2,1,0:T(8,128)}, u32[]{:S(2)}) copy-start(f32[1,16,128]{2,1,0:T(8,128)} %get-tuple-element.69) | copy-start | bytes 24580
  199.2 37.2 %copy-start.67 = (f32[1,1,16]{2,1,0:T(1,128)S(1)}, f32[1,1,16]{2,1,0:T(1,128)}, u32[]{:S(2)}) copy-start(f32[1,1,16]{2,1,0:T(1,128)} %get-tuple-element.75) | copy-start | bytes 196
  199.2 87.3 %all-gather.17.cloned.1.call-start = ((), (), s32[]{:S(2)}) async-start(), calls=%async_computation.6 | async-start | bytes 2621440 | tf_op jit(solution)/shard_map/all_gather | solution.py:37
  249.1 8.6 %copy-start.15 = (bf16[128,1024]{0,1:T(8,128)(2,1)S(1)}, bf16[128,1024]{0,1:T(8,128)(2,1)}, u32[]{:S(2)}) copy-start(bf16[128,1024]{0,1:T(8,128)(2,1)} %get-tuple-element.62) | copy-start | bytes 786436
  286.5 3.9 %copy-start.6 = (f32[128,1,1024]{0,2,1:T(8,128)S(1)}, f32[128,1,1024]{0,2,1:T(8,128)}, u32[]{:S(2)}) copy-start(f32[128,1,1024]{0,2,1:T(8,128)} %copy-done.5) | copy-start | bytes 1572868
  286.5 5.0 %copy-start.12 = (f32[128,1,1024]{0,2,1:T(8,128)S(1)}, f32[128,1,1024]{0,2,1:T(8,128)}, u32[]{:S(2)}) copy-start(f32[128,1,1024]{0,2,1:T(8,128)} %copy.131) | copy-start | bytes 1572868
  290.5 4.3 %copy-start.13 = (f32[128,1024]{0,1:T(8,128)S(1)}, f32[128,1024]{0,1:T(8,128)}, u32[]{:S(2)}) copy-start(f32[128,1024]{0,1:T(8,128)} %get-tuple-element.49) | copy-start | bytes 1572868
  290.5 4.3 %copy-start.30 = (f32[1,16,128]{2,1,0:T(8,128)S(1)}, f32[1,16,128]{2,1,0:T(8,128)}, u32[]{:S(2)}) copy-start(f32[1,16,128]{2,1,0:T(8,128)} %copy-done.28) | copy-start | bytes 24580
  290.5 4.3 %copy-start.32 = (f32[128,128]{1,0:T(8,128)S(1)}, f32[128,128]{1,0:T(8,128)}, u32[]{:S(2)}) copy-start(f32[128,128]{1,0:T(8,128)} %fusion.79) | copy-start | bytes 196612
  290.5 4.3 %copy-start.36 = (f32[128,16]{0,1:T(8,128)S(1)}, f32[128,16]{0,1:T(8,128)}, u32[]{:S(2)}) copy-start(f32[128,16]{0,1:T(8,128)} %copy-done.35) | copy-start | bytes 24580
  290.5 4.3 %copy-start.44 = (pred[128,128]{1,0:T(8,128)(4,1)S(1)}, pred[128,128]{1,0:T(8,128)(4,1)}, u32[]{:S(2)}) copy-start(pred[128,128]{1,0:T(8,128)(4,1)} %fusion.83) | copy-start | bytes 49156
  290.5 4.3 %copy-start.48 = (f32[16,128]{1,0:T(8,128)S(1)}, f32[16,128]{1,0:T(8,128)}, u32[]{:S(2)}) copy-start(f32[16,128]{1,0:T(8,128)} %copy.135) | copy-start | bytes 24580
  297.0 9.7 %copy-start.19 = (f32[128,16]{1,0:T(8,128)S(1)}, f32[128,16]{1,0:T(8,128)}, u32[]{:S(2)}) copy-start(f32[128,16]{1,0:T(8,128)} %copy.158) | copy-start | bytes 24580
  297.0 9.7 %copy-start.20 = (f32[16,128]{0,1:T(8,128)S(1)}, f32[16,128]{0,1:T(8,128)}, u32[]{:S(2)}) copy-start(f32[16,128]{0,1:T(8,128)} %copy.159) | copy-start | bytes 24580
  302.1 12.0 %collective-permute-start.1 = (f32[3,1280]{1,0:T(4,128)}, f32[3,1280]{1,0:T(4,128)}, u32[]{:S(2)}, u32[]{:S(2)}) collective-permute-start(f32[3,1280]{1,0:T(4,128)} %slice.321), channel_id=1, source_target_pairs={{8,0},{16,8},{24,16},{32,24},{40,32},{48,40},{56,48},{64,56},{72,6... | collective-permute-start | bytes 46088 | tf_op jit(solution)/shard_map/ppermute | solution.py:23
  307.7 4.5 %copy-start.66 = (f32[1,16,1]{1,2,0:T(1,128)S(1)}, f32[1,16,1]{1,2,0:T(1,128)}, u32[]{:S(2)}) copy-start(f32[1,16,1]{1,2,0:T(1,128)} %copy-done.65) | copy-start | bytes 196
  307.7 5.0 %copy-start.17 = (f32[16,128]{0,1:T(8,128)S(1)}, f32[16,128]{0,1:T(8,128)}, u32[]{:S(2)}) copy-start(f32[16,128]{0,1:T(8,128)} %copy-done.16) | copy-start | bytes 24580
  307.7 5.0 %copy-start.21 = (f32[1,16,128]{1,2,0:T(8,128)S(1)}, f32[1,16,128]{1,2,0:T(8,128)}, u32[]{:S(2)}) copy-start(f32[1,16,128]{1,2,0:T(8,128)} %copy.156) | copy-start | bytes 24580
  307.7 5.0 %copy-start.22 = (f32[16,128]{0,1:T(8,128)S(1)}, f32[16,128]{0,1:T(8,128)}, u32[]{:S(2)}) copy-start(f32[16,128]{0,1:T(8,128)} %copy.157) | copy-start | bytes 24580
  307.7 5.0 %copy-start.57 = (f32[128]{0:T(128)S(1)}, f32[128]{0:T(128)}, u32[]{:S(2)}) copy-start(f32[128]{0:T(128)} %copy-done.56) | copy-start | bytes 1540
  307.7 5.0 %copy-start.59 = (f32[16]{0:T(128)S(1)}, f32[16]{0:T(128)}, u32[]{:S(2)}) copy-start(f32[16]{0:T(128)} %param.18) | copy-start | bytes 196
  307.7 6.4 %copy-start.25 = (f32[1280]{0:T(1024)S(1)}, f32[1280]{0:T(1024)}, u32[]{:S(2)}) copy-start(f32[1280]{0:T(1024)} %copy-done.24) | copy-start | bytes 15364
  307.7 6.4 %copy-start.27 = (f32[1280]{0:T(1024)S(1)}, f32[1280]{0:T(1024)}, u32[]{:S(2)}) copy-start(f32[1280]{0:T(1024)} %copy-done.26) | copy-start | bytes 15364
  307.7 6.4 %copy-start.60 = (f32[128]{0:T(128)S(1)}, f32[128]{0:T(128)}, u32[]{:S(2)}) copy-start(f32[128]{0:T(128)} %get-tuple-element.87) | copy-start | bytes 1540
  307.8 6.4 %copy-start.61 = (f32[128]{0:T(128)S(1)}, f32[128]{0:T(128)}, u32[]{:S(2)}) copy-start(f32[128]{0:T(128)} %get-tuple-element.88) | copy-start | bytes 1540
  307.8 6.4 %copy-start.62 = (f32[128]{0:T(128)S(1)}, f32[128]{0:T(128)}, u32[]{:S(2)}) copy-start(f32[128]{0:T(128)} %get-tuple-element.89) | copy-start | bytes 1540
  307.8 6.4 %copy-start.63 = (f32[128]{0:T(128)S(1)}, f32[128]{0:T(128)}, u32[]{:S(2)}) copy-start(f32[128]{0:T(128)} %get-tuple-element.90) | copy-start | bytes 1540
  (13 other events, 29.5 us)
Sparse Core Ops, SparseCore 0:
  27.7 17.2 all-gather.18
  47.3 33.6 all-gather.10
  83.7 50.7 all-gather.12
  180.9 15.9 all-gather.20
  199.3 33.6 all-gather.14
  235.7 50.7 all-gather.16
where the time goes:
time: 326 us; the launch traced here: 324 us
  waiting for transfers between devices  140 us (43%)
  other arithmetic  54.5 us (17%)
  blocking collectives  50.2 us (15%)
  local copies, waits for them, and re-layouts  27.5 us (8%)
  matrix products  23.1 us (7%)
  between operations  16.4 us (5%)
  starting transfers between devices  12.4 us (4%)
    all_gather x6, waiting for transfers between devices, carried_in(): pieces = jax.tree.map(lambda part: lax.all_gather(part, axis), subtotal)  140 us
    all_gather x4, blocking collectives, carried_in(): pieces = jax.tree.map(lambda part: lax.all_gather(part, axis), subtotal)  31.3 us
    all_to_all x2, blocking collectives, sent_to_all(): return lax.all_to_all(copies, axis, split_axis=0, concat_axis=0, tiled=True)  18.9 us
    add x6, other arithmetic, compose(): later[0][..., None, None] * earlier[1] + later[1]  16.3 us
    unnamed x141, local copies, waits for them, and re-layouts  8.48 us
    ppermute x2, starting transfers between devices, from_behind(): return lax.ppermute(shard, axis, pairs)  8.27 us
  transfers between devices with their start and end apart: 9, of which 6 were waited for; matrix products, arithmetic and copies ran while one was open for 16% of the time, Pallas kernels for 0%

commit v1 on v0

v1 whole, which is shorter than its diff:
```python
import functools

import jax
import jax.numpy as jnp
from jax import lax
from jax.experimental import pallas as pl
from jax.experimental.pallas import tpu as pltpu
from jax.sharding import PartitionSpec as P

HEADS = 128
HEAD_DIM = 64
STATE = 128
GROUPS = 8
TAPS = 4
LBLK = 64
DOCS = 8
D_INNER = 8192
GROUP_WIDTH = 1024
ROWS = 128
PAIRS = 8
TILES = 10
MSG = 136
CHIPS = 4
NCTX = 32
NTP = 8
MESH = pl.DeviceIdType.MESH
F32 = jnp.float32
BF16 = jnp.bfloat16


def split(value):
    high = value.astype(BF16)
    return high, (value - high.astype(F32)).astype(BF16)


def one_pass(left, right, dims):
    return lax.dot_general(
        left, right, (((dims[0],), (dims[1],)), ((), ())), preferred_element_type=F32
    )


def product(left, right, dims=(1, 0)):
    left_high, left_low = left
    right_high, right_low = right
    return one_pass(left_high, right_high, dims) + (
        one_pass(left_high, right_low, dims) + one_pass(left_low, right_high, dims)
    )


def summed_by(value, ones):
    high = value.astype(BF16)
    rest = value - high.astype(F32)
    middle = rest.astype(BF16)
    low = (rest - middle.astype(F32)).astype(BF16)
    return one_pass(high, ones, (1, 0)) + (
        one_pass(middle, ones, (1, 0)) + one_pass(low, ones, (1, 0))
    )


def sigmoid(value):
    return 1.0 / (1.0 + jnp.exp(-value))


def tall(row):
    return jnp.broadcast_to(row, (ROWS, ROWS))


def two_heads(first, second):
    stacked = jnp.concatenate(
        [jnp.broadcast_to(first, (64, ROWS)), jnp.broadcast_to(second, (64, ROWS))], axis=0
    )
    return stacked.T


def kernel(
    labels,
    doc_lengths,
    conv_input,
    gate_input,
    dt_raw,
    conv_weight,
    conv_bias,
    dt_bias,
    a_log,
    norm_gain,
    reference_out,
    out_input,
    out_gate,
    out_dt,
    rim,
    ext,
    act,
    slope,
    w_out_x,
    w_in_x,
    weighted,
    decay,
    mix,
    inner,
    read,
    gate_act,
    gate_slope,
    grad_y,
    grad_in,
    carried,
    adjoint,
    grad_x,
    grad_pre,
    rim_out,
    rim_in,
    scores,
    mask,
    bc,
    grad_scores,
    grad_b,
    grad_c,
    sums,
    table,
    totals,
    msg_f,
    near_f,
    chip_f,
    row_f,
    zin_f,
    zout_f,
    back_f,
    own_f,
    other_f,
    msg_b,
    near_b,
    chip_b,
    row_b,
    zin_b,
    zout_b,
    back_b,
    own_b,
    other_b,
    send_sem,
    recv_sem,
):
    ctx = lax.axis_index("ctx")
    tp = lax.axis_index("tp")
    core = lax.rem(ctx, 2)
    xpos = lax.rem(ctx // 2, CHIPS)
    zpos = ctx // (2 * CHIPS)
    partner = ctx + 1 - 2 * core
    after = lax.rem(ctx + 1, NCTX)
    before = lax.rem(ctx + NCTX - 1, NCTX)

    def chip_at(z, x):
        return (z * CHIPS + x) * 2 + core

    barrier = pltpu.get_barrier_semaphore()
    peers = [(partner, tp), (after, tp), (before, tp)]
    for step in range(1, CHIPS):
        peers.append((chip_at(zpos, lax.rem(xpos + step, CHIPS)), tp))
    peers.append((chip_at(lax.rem(zpos + 1, 4), xpos), tp))
    peers.append((chip_at(lax.rem(zpos + 3, 4), xpos), tp))
    for step in range(1, NTP):
        peers.append((ctx, lax.rem(tp + step, NTP)))
    for peer in peers:
        pl.semaphore_signal(barrier, inc=1, device_id=peer, device_id_type=MESH)

    def copy(src, dst, sem, peer):
        return pltpu.make_async_remote_copy(
            src_ref=src,
            dst_ref=dst,
            send_sem=send_sem.at[sem],
            recv_sem=recv_sem.at[sem],
            device_id=peer,
            device_id_type=MESH,
        )

    row_index = lax.broadcasted_iota(jnp.int32, (ROWS, ROWS), 0)
    lane_index = lax.broadcasted_iota(jnp.int32, (ROWS, ROWS), 1)
    first_half = lane_index < 64
    first_pos = ctx * ROWS
    starts = []
    so_far = jnp.int32(0)
    for d in range(DOCS):
        starts.append(so_far)
        so_far = so_far + doc_lengths[d]

    def doc_of(position):
        found = jnp.full_like(position, -1)
        for start in starts:
            found = found + jnp.where(start <= position, 1, 0)
        return found

    docs_down = doc_of(first_pos + row_index)
    docs_across = doc_of(first_pos + lane_index)
    docs_row = docs_across[0:1, :]
    prev_doc = doc_of(jnp.full((1, ROWS), first_pos - 1, jnp.int32))
    last_doc = doc_of(jnp.full((1, ROWS), first_pos + ROWS - 1, jnp.int32))
    mask[...] = jnp.where((row_index >= lane_index) & (docs_down == docs_across), 1.0, 0.0)
    keep_out = jnp.where(docs_row == last_doc, 1.0, 0.0)
    keep_in = jnp.where(docs_row == prev_doc, 1.0, 0.0)
    through = jnp.where(prev_doc == last_doc, 1.0, 0.0)

    eye = (
        lax.broadcasted_iota(jnp.int32, (16, 16), 0) == lax.broadcasted_iota(jnp.int32, (16, 16), 1)
    )

    def down(row):
        return jnp.sum(jnp.where(eye, jnp.broadcast_to(row, (16, 16)), 0.0), axis=1, keepdims=True)

    shifted = dt_raw[...] + down(dt_bias[...])
    rate = jnp.exp(down(a_log[...]))
    small = jnp.exp(-jnp.abs(shifted))
    step_size = jnp.maximum(shifted, 0.0) + jnp.log1p(small)
    ones_upper = jnp.where(row_index <= lane_index, 1.0, 0.0).astype(BF16)
    log_cumul = summed_by(-rate * step_size, ones_upper)
    log_end = log_cumul[:, ROWS - 1 : ROWS]
    ends = jnp.exp(log_end - log_cumul) * keep_out
    w_out = ends * step_size
    w_in = jnp.exp(log_cumul) * keep_in
    passing = jnp.broadcast_to(jnp.exp(log_end), (16, ROWS)) * through
    LOG, STEP, ENDS, WOUT, WIN, PASS, CUM, GSTEP, GWEIGHT, GEND = range(10)
    table[LOG] = log_cumul
    table[STEP] = step_size
    table[ENDS] = ends
    table[WOUT] = w_out
    table[WIN] = w_in
    table[PASS] = passing

    pl.semaphore_wait(barrier, len(peers))
    rim_copy = copy(conv_input.at[ROWS - 16 : ROWS], rim, 0, (after, tp))
    rim_copy.start()

    def lanes(i):
        return pl.ds(pl.multiple_of(i * ROWS, ROWS), ROWS)

    def row_of(which, h):
        return table[which, pl.ds(h, 1), :]

    def expand(j, carry):
        w_out_x[j] = two_heads(row_of(WOUT, 2 * j), row_of(WOUT, 2 * j + 1))
        w_in_x[j] = two_heads(row_of(WIN, 2 * j), row_of(WIN, 2 * j + 1))
        lane_row = lax.broadcasted_iota(jnp.int32, (1, ROWS), 1)
        pass_row = jnp.where(lane_row < 64, row_of(PASS, 2 * j), row_of(PASS, 2 * j + 1))
        pass_rows = jnp.broadcast_to(pass_row, (8, ROWS))
        msg_f[j, ROWS:MSG, :] = pass_rows
        msg_b[j, ROWS:MSG, :] = pass_rows
        return carry

    lax.fori_loop(0, PAIRS, expand, 0)

    same_before = [
        jnp.where(doc_of(first_pos + row_index - o) == docs_down, 1.0, 0.0) for o in range(1, TAPS)
    ]
    same_after = [
        jnp.where(doc_of(first_pos + row_index + o) == docs_down, 1.0, 0.0) for o in range(1, TAPS)
    ]

    rim_copy.wait_recv()

    def convolve(i, carry):
        ext[i, 8:MSG, :] = conv_input[:, lanes(i)].astype(F32)
        ext[i, 0:8, :] = rim[:, lanes(i)].astype(F32)[8:16]
        pre = conv_bias[:, lanes(i)] + conv_weight[TAPS - 1 : TAPS, lanes(i)] * ext[i, 8:MSG, :]
        for o in range(1, TAPS):
            tap = conv_weight[TAPS - 1 - o : TAPS - o, lanes(i)]
            pre = pre + tap * ext[i, 8 - o : MSG - o, :] * same_before[o - 1]
        sigma = sigmoid(pre)
        act[i] = pre * sigma
        slope[i] = sigma * (1.0 + pre * (1.0 - sigma))
        return carry

    lax.fori_loop(0, TILES, convolve, 0)

    b_rows = act[PAIRS]
    c_rows = act[PAIRS + 1]
    b_high, b_low = split(b_rows)
    c_high, c_low = split(c_rows)
    bc[0], bc[1], bc[2], bc[3] = b_high, b_low, c_high, c_low
    bt_high, bt_low = split(b_rows.T)
    ct_high, ct_low = split(c_rows.T)
    bc[4], bc[5], bc[6], bc[7] = bt_high, bt_low, ct_high, ct_low

    def local_state(j, carry):
        part = act[j] * w_out_x[j]
        weighted[j] = part
        msg_f[j, 0:ROWS, :] = product((bc[4], bc[5]), split(part))
        return carry

    theirs = (1 - core) * CHIPS
    mine = core * CHIPS

    def within(j, carry):
        x_pair = split(act[j])
        parts = []
        for half in range(2):
            h = 2 * j + half
            across = tall(row_of(LOG, h))
            gap = across.T - across
            matrix = jnp.exp(jnp.where(mask[...] > 0.0, gap, -1e30))
            decay[h] = matrix
            mixed = scores[...] * matrix * row_of(STEP, h)
            mix[h] = mixed
            parts.append(product(split(mixed), x_pair))
        inner[j] = jnp.where(first_half, parts[0], parts[1])
        gate = gate_input[:, lanes(j)].astype(F32)
        sigma = sigmoid(gate)
        gate_act[j] = gate * sigma
        gate_slope[j] = sigma * (1.0 + gate * (1.0 - sigma))
        return carry

    def scan(buffers, base, reverse, fill, work, result):
        msg, near, chip, row, zin, zout, back, own, other = buffers
        lax.fori_loop(theirs, theirs + CHIPS, fill, 0)
        near_copy = copy(msg.at[pl.ds(theirs, CHIPS)], near, base, (partner, tp))
        near_copy.start()
        lax.fori_loop(mine, mine + CHIPS, fill, 0)
        near_copy.wait_recv()
        is_first = core == (1 if reverse else 0)

        def combine(q, carry):
            my_pass = msg[mine + q, ROWS : ROWS + 1, :]
            their_pass = near[q, ROWS : ROWS + 1, :]
            my_scale = jnp.where(is_first, their_pass, 1.0)
            their_scale = jnp.where(is_first, 1.0, my_pass)
            chip[q, 0:ROWS, :] = (
                msg[mine + q, 0:ROWS, :] * my_scale + near[q, 0:ROWS, :] * their_scale
            )
            chip[q, ROWS:MSG, :] = jnp.broadcast_to(my_pass * their_pass, (8, ROWS))
            return carry

        lax.fori_loop(0, CHIPS, combine, 0)
        across = []
        for step in range(1, CHIPS):
            there = lax.rem(xpos + step, CHIPS)
            across.append(
                copy(chip.at[there], row.at[xpos], base + step, (chip_at(zpos, there), tp))
            )
            across[-1].start()
        row[xpos] = chip[xpos]
        for each in across:
            each.wait_recv()
        order = list(range(CHIPS))
        if reverse:
            order = order[::-1]
        order_pass = jnp.ones((1, ROWS), F32)
        running = None
        back_scale = []
        for place, x in enumerate(order):
            back_scale.append(order_pass)
            here_pass = row[x, ROWS : ROWS + 1, :]
            if place == 0:
                running = row[x, 0:ROWS, :]
            else:
                back[x] = running
                running = running * here_pass + row[x, 0:ROWS, :]
            order_pass = order_pass * here_pass
        zout[...] = running
        at_start = zpos == (3 if reverse else 0)
        at_end = zpos == (0 if reverse else 3)
        rank = 3 - zpos if reverse else zpos
        early = (rank * PAIRS) // 3
        up = chip_at(jnp.maximum(zpos - 1, 0) if reverse else jnp.minimum(zpos + 1, 3), xpos)
        lax.fori_loop(0, early, work, 0)

        @pl.when(jnp.logical_not(at_start))
        def _():
            copy(zout, zin, base + 4, (up, tp)).wait_recv()
            zout[...] = zout[...] + zin[...] * order_pass

        @pl.when(at_start)
        def _():
            zin[...] = jnp.zeros((ROWS, ROWS), F32)

        @pl.when(jnp.logical_not(at_end))
        def _():
            copy(zout, zin, base + 4, (up, tp)).start()

        for place, x in enumerate(order):
            if place == 0:
                back[x] = zin[...]
            else:
                back[x] = back[x] + zin[...] * back_scale[place]
        returned = []
        for step in range(1, CHIPS):
            there = lax.rem(xpos + step, CHIPS)
            returned.append(
                copy(back.at[there], own.at[xpos], base + 4 + step, (chip_at(zpos, there), tp))
            )
            returned[-1].start()
        own[xpos] = back[xpos]
        lax.fori_loop(early, PAIRS, work, 0)
        for each in returned:
            each.wait_recv()

        def spread(q, carry):
            my_pass = msg[mine + q, ROWS : ROWS + 1, :]
            their_pass = near[q, ROWS : ROWS + 1, :]
            entering = own[q]
            one = jnp.ones((1, ROWS), F32)
            zero = jnp.zeros((1, ROWS), F32)
            other[q] = entering * jnp.where(is_first, my_pass, one) + msg[
                mine + q, 0:ROWS, :
            ] * jnp.where(is_first, one, zero)
            result[mine + q] = entering * jnp.where(is_first, one, their_pass) + near[
                q, 0:ROWS, :
            ] * jnp.where(is_first, zero, one)
            return carry

        lax.fori_loop(0, CHIPS, spread, 0)
        last = copy(other, result.at[pl.ds(mine, CHIPS)], base + 8, (partner, tp))
        last.start()
        last.wait_recv()

        def drain():
            near_copy.wait_send()
            for each in across + returned:
                each.wait_send()
            last.wait_send()

            @pl.when(jnp.logical_not(at_end))
            def _():
                copy(zout, zin, base + 4, (up, tp)).wait_send()

        return drain

    def fill_forward(j, carry):
        return local_state(j, carry)

    scores[...] = product((c_high, c_low), (b_high, b_low), (1, 1))
    forward = (msg_f, near_f, chip_f, row_f, zin_f, zout_f, back_f, own_f, other_f)
    drain_forward = scan(forward, 1, False, fill_forward, within, carried)

    sums[...] = jnp.zeros((4, ROWS, ROWS), F32)

    def outputs(j, carry):
        part = product((bc[2], bc[3]), split(carried[j])) * w_in_x[j]
        read[j] = part
        total = inner[j] + part
        inner[j] = total
        gated = total * gate_act[j]
        gained = gated * norm_gain[:, lanes(j)]
        target = reference_out[:, lanes(j)].astype(F32)
        sums[0] = sums[0] + gated * gated
        sums[1] = sums[1] + gained * target
        sums[2] = sums[2] + gained * gained
        sums[3] = sums[3] + target * target
        return carry

    lax.fori_loop(0, PAIRS, outputs, 0)
    square = jnp.sum(sums[0].T, axis=0, keepdims=True) / GROUP_WIDTH + 1e-05
    dot_here = jnp.sum(sums[1].T, axis=0, keepdims=True)
    self_here = jnp.sum(sums[2].T, axis=0, keepdims=True)
    ref_here = jnp.sum(sums[3].T, axis=0, keepdims=True)
    inverse = lax.rsqrt(square)
    inverse = inverse * (1.5 - 0.5 * square * inverse * inverse)
    totals[tp] = jnp.concatenate(
        [
            dot_here * inverse,
            self_here * inverse * inverse,
            ref_here,
            jnp.zeros((5, ROWS), F32),
        ],
        axis=0,
    )
    tp_copies = []
    for step in range(1, NTP):
        there = lax.rem(tp + step, NTP)
        tp_copies.append(copy(totals.at[tp], totals.at[tp], 18 + step, (ctx, there)))
        tp_copies[-1].start()
    for each in tp_copies:
        each.wait_recv()
    total = totals[0]
    for k in range(1, NTP):
        total = total + totals[k]
    mean_all = total / D_INNER
    mean_dot, mean_self, mean_ref = mean_all[0:1], mean_all[1:2], mean_all[2:3]
    norm_self = jnp.sqrt(mean_self + 1e-06)
    norm_ref = jnp.sqrt(mean_ref + 1e-06)
    cosine = mean_dot / (norm_self * norm_ref)
    distance = jnp.sqrt(mean_self - 2.0 * mean_dot + mean_ref + 1e-06)
    lane_row = lax.broadcasted_iota(jnp.int32, (1, ROWS), 1)
    harmful = jnp.where(lane_row < LBLK, labels[0], labels[1]).astype(F32)
    coef_self = -harmful * cosine / (norm_self * norm_self) + (1.0 - harmful) / distance
    coef_ref = harmful / (norm_self * norm_ref) - (1.0 - harmful) / distance
    mean_scaled = (coef_self * inverse * self_here + coef_ref * dot_here) / GROUP_WIDTH
    sums[0] = tall(coef_self * inverse * inverse).T
    sums[1] = tall(mean_scaled * inverse * inverse * inverse).T
    sums[2] = tall(coef_ref * inverse).T

    def fill_backward(j, carry):
        gain = norm_gain[:, lanes(j)]
        target = reference_out[:, lanes(j)].astype(F32)
        mixer_out = inner[j]
        gate = gate_act[j]
        gated = mixer_out * gate
        flow = gated * (sums[0] * (gain * gain) - sums[1]) + sums[2] * (gain * target)
        out_gate[:, lanes(j)] = (flow * mixer_out * gate_slope[j]).astype(BF16)
        into = flow * gate
        grad_y[j] = into
        entering = into * w_in_x[j]
        grad_in[j] = entering
        msg_b[j, 0:ROWS, :] = product((bc[6], bc[7]), split(entering))
        return carry

    grad_scores[...] = jnp.zeros((ROWS, ROWS), F32)
    grad_b[...] = jnp.zeros((ROWS, ROWS), F32)
    grad_c[...] = jnp.zeros((ROWS, ROWS), F32)

    def halves(value):
        turned = value.T
        return (
            jnp.sum(turned[0:64], axis=0, keepdims=True),
            jnp.sum(turned[64:128], axis=0, keepdims=True),
        )

    def within_back(j, carry):
        x_pair = split(act[j])
        flow = grad_y[j]
        flow_pair = split(flow)
        by_read = halves(read[j] * flow)
        parts = []
        for half in range(2):
            h = 2 * j + half
            picked = first_half if half == 0 else jnp.logical_not(first_half)
            only = split(jnp.where(picked, flow, 0.0))
            via = product(only, x_pair, (1, 1)) * decay[h]
            step_row = row_of(STEP, h)
            grad_scores[...] = grad_scores[...] + via * step_row
            scored = via * scores[...]
            by_step = jnp.sum(scored, axis=0, keepdims=True)
            table[GSTEP, pl.ds(h, 1), :] = by_step
            across = jnp.sum((scored * step_row).T, axis=0, keepdims=True)
            table[CUM, pl.ds(h, 1), :] = across - by_step * step_row + by_read[half]
            parts.append(product(split(mix[h].T), flow_pair))
        grad_x[j] = jnp.where(first_half, parts[0], parts[1])
        grad_c[...] = grad_c[...] + product(split(grad_in[j]), split(carried[j]), (1, 1))
        return carry

    backward = (msg_b, near_b, chip_b, row_b, zin_b, zout_b, back_b, own_b, other_b)
    drain_backward = scan(backward, 10, True, fill_backward, within_back, adjoint)

    def finish(j, carry):
        coming = adjoint[j]
        coming_pair = split(coming)
        later = product((bc[0], bc[1]), coming_pair)
        grad = grad_x[j] + later * w_out_x[j]
        grad_pre[j, 0:ROWS, :] = grad * slope[j]
        rim_out[j] = grad_pre[j, 0:8, :]
        by_weight = halves(later * act[j])
        table[GWEIGHT, pl.ds(2 * j, 1), :] = by_weight[0]
        table[GWEIGHT, pl.ds(2 * j + 1, 1), :] = by_weight[1]
        ended = jnp.sum(carried[j] * coming, axis=0, keepdims=True)
        table[GEND, pl.ds(2 * j, 1), :] = jnp.where(lane_row < 64, ended, 0.0)
        table[GEND, pl.ds(2 * j + 1, 1), :] = jnp.where(lane_row < 64, 0.0, ended)
        grad_b[...] = grad_b[...] + product(split(weighted[j]), coming_pair, (1, 1))
        return carry

    lax.fori_loop(0, PAIRS, finish, 0)
    via_scores = grad_scores[...]
    by_b = grad_b[...] + product(split(via_scores.T), (bc[2], bc[3]))
    by_c = grad_c[...] + product(split(via_scores), (bc[0], bc[1]))
    grad_pre[PAIRS, 0:ROWS, :] = by_b * slope[PAIRS]
    grad_pre[PAIRS + 1, 0:ROWS, :] = by_c * slope[PAIRS + 1]
    rim_out[PAIRS] = grad_pre[PAIRS, 0:8, :]
    rim_out[PAIRS + 1] = grad_pre[PAIRS + 1, 0:8, :]
    rim_back = copy(rim_out, rim_in, 26, (before, tp))
    rim_back.start()

    grad_weight = table[GWEIGHT]
    leaving = grad_weight * table[WOUT]
    at_end = jnp.sum(leaving, axis=1, keepdims=True) + jnp.sum(
        table[GEND] * table[PASS], axis=1, keepdims=True
    )
    lane_16 = lax.broadcasted_iota(jnp.int32, (16, ROWS), 1)
    grad_cum = table[CUM] - leaving + jnp.where(lane_16 == ROWS - 1, at_end, 0.0)
    ones_lower = jnp.where(row_index >= lane_index, 1.0, 0.0).astype(BF16)
    grad_log = summed_by(grad_cum, ones_lower)
    grad_step = grad_weight * table[ENDS] + table[GSTEP]
    shifted_again = dt_raw[...] + down(dt_bias[...])
    rate_again = jnp.exp(down(a_log[...]))
    out_dt[...] = (grad_step - rate_again * grad_log) * sigmoid(shifted_again)

    drain_forward()
    rim_copy.wait_send()
    for each in tp_copies:
        each.wait_send()
    rim_back.wait_recv()
    inside = jnp.where(ctx == NCTX - 1, 0.0, 1.0)

    def spread_taps(i, carry):
        grad_pre[i, ROWS:MSG, :] = rim_in[i] * inside
        total = conv_weight[TAPS - 1 : TAPS, lanes(i)] * grad_pre[i, 0:ROWS, :]
        for o in range(1, TAPS):
            tap = conv_weight[TAPS - 1 - o : TAPS - o, lanes(i)]
            total = total + tap * grad_pre[i, o : ROWS + o, :] * same_after[o - 1]
        out_input[:, lanes(i)] = total.astype(BF16)
        return carry

    lax.fori_loop(0, TILES, spread_taps, 0)
    drain_backward()
    rim_back.wait_send()


def on_device(
    conv_input,
    gate_input,
    dt_raw,
    conv_weight,
    conv_bias,
    dt_bias,
    a_log,
    norm_gain,
    reference_out,
    labels,
    doc_lengths,
):
    square = (ROWS, ROWS)
    by_pair = pltpu.VMEM((PAIRS, *square), F32)
    by_tile = pltpu.VMEM((TILES, *square), F32)
    padded = pltpu.VMEM((TILES, MSG, ROWS), F32)
    one = pltpu.VMEM(square, F32)
    scans = [
        pltpu.VMEM((PAIRS, MSG, ROWS), F32),
        pltpu.VMEM((CHIPS, MSG, ROWS), F32),
        pltpu.VMEM((CHIPS, MSG, ROWS), F32),
        pltpu.VMEM((CHIPS, MSG, ROWS), F32),
        one,
        one,
        pltpu.VMEM((CHIPS, *square), F32),
        pltpu.VMEM((CHIPS, *square), F32),
        pltpu.VMEM((CHIPS, *square), F32),
    ]
    vmem = pl.BlockSpec(memory_space=pltpu.VMEM)
    smem = pl.BlockSpec(memory_space=pltpu.SMEM)
    scratch = [
        pltpu.VMEM((16, TILES * ROWS), BF16),
        padded,
        by_tile,
        by_tile,
        by_pair,
        by_pair,
        by_pair,
        pltpu.VMEM((16, *square), F32),
        pltpu.VMEM((16, *square), F32),
        by_pair,
        by_pair,
        by_pair,
        by_pair,
        by_pair,
        by_pair,
        by_pair,
        by_pair,
        by_pair,
        padded,
        pltpu.VMEM((TILES, 8, ROWS), F32),
        pltpu.VMEM((TILES, 8, ROWS), F32),
        one,
        one,
        pltpu.VMEM((8, *square), BF16),
        one,
        one,
        one,
        pltpu.VMEM((4, *square), F32),
        pltpu.VMEM((10, 16, ROWS), F32),
        pltpu.VMEM((NTP, 8, ROWS), F32),
        *scans,
        *scans,
        pltpu.SemaphoreType.DMA((27,)),
        pltpu.SemaphoreType.DMA((27,)),
    ]
    return pl.pallas_call(
        kernel,
        out_shape=(
            jax.ShapeDtypeStruct(conv_input.shape, BF16),
            jax.ShapeDtypeStruct(gate_input.shape, BF16),
            jax.ShapeDtypeStruct(dt_raw.shape, F32),
        ),
        in_specs=[smem] * 2 + [vmem] * 9,
        out_specs=(vmem, vmem, vmem),
        scratch_shapes=scratch,
        compiler_params=pltpu.CompilerParams(
            collective_id=0, has_side_effects=True, vmem_limit_bytes=60 * 1024 * 1024
        ),
    )(
        labels,
        doc_lengths,
        conv_input,
        gate_input,
        dt_raw,
        conv_weight,
        conv_bias.reshape(1, -1),
        dt_bias.reshape(1, -1),
        a_log.reshape(1, -1),
        norm_gain.reshape(1, -1),
        reference_out,
    )


def solution(mesh):
    in_specs = (
        P("ctx", "tp"),
        P("ctx", "tp"),
        P("tp", "ctx"),
        P(None, "tp"),
        P("tp"),
        P("tp"),
        P("tp"),
        P("tp"),
        P("ctx", "tp"),
        P("ctx"),
        P(),
    )
    out_specs = (P("ctx", "tp"), P("ctx", "tp"), P("tp", "ctx"))
    return jax.shard_map(
        on_device, mesh=mesh, in_specs=in_specs, out_specs=out_specs, check_vma=False
    )
```

time: 326 us -> 85.1 us (0.26)
  waiting for transfers between devices: 140 us -> 0 us
  Pallas kernels: 0 us -> 79.9 us
  other arithmetic: 54.5 us -> 0 us
  blocking collectives: 50.2 us -> 0 us
  local copies, waits for them, and re-layouts: 27.5 us -> 4.36 us
  matrix products: 23.1 us -> 0 us
  between operations: 16.4 us -> 0.65 us
  starting transfers between devices: 12.4 us -> 0 us
    all_gather x6 -> x0, waiting for transfers between devices: 140 us -> none  [carried_in(): pieces = jax.tree.map(lambda part: lax.all_gather(part, axis), subtotal)]
    pallas_call x0 -> x1, Pallas kernels: none -> 79.9 us  [on_device(): pl.pallas_call(kernel, out_shape=(jax.ShapeDtypeStruct(conv_input.shape,...]
    all_gather x4 -> x0, blocking collectives: 31.3 us -> none  [carried_in(): pieces = jax.tree.map(lambda part: lax.all_gather(part, axis), subtotal)]
    dot_general x12 -> x0, matrix products: 23.1 us -> none  [the longest x1 4.36 us: on_device(): grad_mix = jnp.einsum('tgjp,sgjp->gjts', grad_mixer, x_part, precision=HIGH)]
    all_to_all x2 -> x0, blocking collectives: 18.9 us -> none  [sent_to_all(): return lax.all_to_all(copies, axis, split_axis=0, concat_axis=0, tiled=True)]
    add x11 -> x0, other arithmetic: 17 us -> none  [the longest x6 16.3 us: compose(): later[0][..., None, None] * earlier[1] + later[1]]
    reduce_sum x12 -> x0, other arithmetic: 13.4 us -> none  [the longest x1 4.33 us: on_device(): jnp.sum(carried * adjoint, axis=(2, 3)) * pass_part]
    mul x13 -> x0, other arithmetic: 11 us -> none  [the longest x3 3.06 us: compose(): earlier[0] * later[0]]
  transfers between devices with their start and end apart: 9 -> 0, of which waited for: 6 -> 0; matrix products, arithmetic and copies ran while one was open for 16% -> 0% of each run, Pallas kernels for 0% -> 0%
where the time goes in v1:
time: 85.1 us; the launch traced here: 84.9 us
  Pallas kernels  79.9 us (94%)
  local copies, waits for them, and re-layouts  4.36 us (5%)
    pallas_call x1, Pallas kernels, on_device(): pl.pallas_call(kernel, out_shape=(jax.ShapeDtypeStruct(conv_input.shape,...  79.9 us
    unnamed x7, local copies, waits for them, and re-layouts  3.07 us

profile of v1, /device:TPU:1, one launch (start us, length us, event | category | flops | bytes accessed | tf_op | source)
XLA Modules:
  0.0 84.9 jit_solution(17121368281932170069)
XLA Ops:
  0.6 1.3 %reshape.18.conv_bias = f32[1,1280]{1,0:T(1,128)} reshape(f32[1280]{0:T(1024)} %param.15) | data formatting | bytes 10240 | tf_op jit(solution)/shard_map/reshape | solution.py:688
  1.9 79.9 %shard_map.130 = (bf16[128,1280]{1,0:T(8,128)(2,1)}, bf16[128,1024]{1,0:T(8,128)(2,1)}, f32[16,128]{1,0:T(8,128)}) custom-call(s32[2]{0:T(128)} %labels.1, s32[8]{0:T(128)} %doc_lengths.1, bf16[128,1280]{1,0:T(8,128)(2,1)} %conv_input.1, bf16[128,1024]{1,0:T(8,128)(2,1)} %gate_input.1, f32[16,128]{1,0:T(8,128)} %dt_raw.1, f32[4,1280]{1,0:T(4,128)} %conv_weight.1, ...), custom_call_target="tpu_custom_call" | custom-call | tf_op jit(solution)/shard_map/pallas_call | solution.py:668
  81.8 0.0 copy-start
  81.8 1.8 %copy.17 = bf16[128,1280]{1,0:T(8,128)(2,1)} copy(bf16[128,1280]{1,0:T(8,128)(2,1)} %get-tuple-element.6) | data formatting | bytes 655360
  83.6 0.0 copy-done
  83.6 0.0 copy-start.1
  83.6 0.7 copy.18
  84.3 0.0 copy-done.1
  84.3 0.6 copy.19
Async XLA Ops:
  81.8 1.8 %copy-start = (bf16[128,1024]{1,0:T(8,128)(2,1)S(1)}, bf16[128,1024]{1,0:T(8,128)(2,1)}, u32[]{:S(2)}) copy-start(bf16[128,1024]{1,0:T(8,128)(2,1)} %get-tuple-element.7) | copy-start | bytes 786436
  83.6 0.7 copy-start.1

commit v2 on v1

--- a/solution.py
+++ b/solution.py
@@ -20,7 +20,13 @@
 PAIRS = 8
 TILES = 10
 MSG = 136
+HEAD = 8
+CHUNKS = 4
+PIECE = ROWS // CHUNKS
+SOON = 4
+EARLY = 4
 CHIPS = 4
+SCAN_SEMS = CHIPS + 9 * CHUNKS
 NCTX = 32
 NTP = 8
 MESH = pl.DeviceIdType.MESH
@@ -73,6 +79,20 @@
 
 
 def kernel(
+    labels_hbm,
+    doc_lengths_hbm,
+    conv_input_hbm,
+    gate_input_hbm,
+    dt_raw_hbm,
+    conv_weight_hbm,
+    conv_bias_hbm,
+    dt_bias_hbm,
+    a_log_hbm,
+    norm_gain_hbm,
+    reference_out_hbm,
+    out_input,
+    out_gate,
+    out_dt,
     labels,
     doc_lengths,
     conv_input,
@@ -84,9 +104,7 @@
     a_log,
     norm_gain,
     reference_out,
-    out_input,
-    out_gate,
-    out_dt,
+    bias,
     rim,
     ext,
     act,
@@ -111,6 +129,7 @@
     scores,
     mask,
     bc,
+    arriving,
     grad_scores,
     grad_b,
     grad_c,
@@ -123,6 +142,7 @@
     row_f,
     zin_f,
     zout_f,
+    zfar_f,
     back_f,
     own_f,
     other_f,
@@ -132,11 +152,13 @@
     row_b,
     zin_b,
     zout_b,
+    zfar_b,
     back_b,
     own_b,
     other_b,
     send_sem,
     recv_sem,
+    load_sem,
 ):
     ctx = lax.axis_index("ctx")
     tp = lax.axis_index("tp")
@@ -161,6 +183,29 @@
     for peer in peers:
         pl.semaphore_signal(barrier, inc=1, device_id=peer, device_id_type=MESH)
 
+    loads = {}
+    for place, (name, src, dst) in enumerate(
+        (
+            ("labels", labels_hbm, labels),
+            ("doc_lengths", doc_lengths_hbm, doc_lengths),
+            ("conv_input", conv_input_hbm, conv_input),
+            ("gate_input", gate_input_hbm, gate_input),
+            ("dt_raw", dt_raw_hbm, dt_raw),
+            ("conv_weight", conv_weight_hbm, conv_weight),
+            ("conv_bias", conv_bias_hbm, conv_bias),
+            ("dt_bias", dt_bias_hbm, dt_bias),
+            ("a_log", a_log_hbm, a_log),
+            ("norm_gain", norm_gain_hbm, norm_gain),
+            ("reference_out", reference_out_hbm, reference_out),
+        )
+    ):
+        loads[name] = pltpu.make_async_copy(src, dst, load_sem.at[place])
+        loads[name].start()
+
+    def arrived(*which):
+        for name in which:
+            loads[name].wait()
+
     def copy(src, dst, sem, peer):
         return pltpu.make_async_remote_copy(
             src_ref=src,
@@ -175,6 +220,7 @@
     lane_index = lax.broadcasted_iota(jnp.int32, (ROWS, ROWS), 1)
     first_half = lane_index < 64
     first_pos = ctx * ROWS
+    arrived("doc_lengths", "labels", "dt_raw", "dt_bias", "a_log")
     starts = []
     so_far = jnp.int32(0)
     for d in range(DOCS):
@@ -223,6 +269,7 @@
     table[WIN] = w_in
     table[PASS] = passing
 
+    arrived("conv_input")
     pl.semaphore_wait(barrier, len(peers))
     rim_copy = copy(conv_input.at[ROWS - 16 : ROWS], rim, 0, (after, tp))
     rim_copy.start()
@@ -239,8 +286,8 @@
         lane_row = lax.broadcasted_iota(jnp.int32, (1, ROWS), 1)
         pass_row = jnp.where(lane_row < 64, row_of(PASS, 2 * j), row_of(PASS, 2 * j + 1))
         pass_rows = jnp.broadcast_to(pass_row, (8, ROWS))
-        msg_f[j, ROWS:MSG, :] = pass_rows
-        msg_b[j, ROWS:MSG, :] = pass_rows
+        msg_f[j, 0:HEAD, :] = pass_rows
+        msg_b[j, 0:HEAD, :] = pass_rows
         return carry
 
     lax.fori_loop(0, PAIRS, expand, 0)
@@ -252,12 +299,14 @@
         jnp.where(doc_of(first_pos + row_index + o) == docs_down, 1.0, 0.0) for o in range(1, TAPS)
     ]
 
-    rim_copy.wait_recv()
+    arrived("conv_bias", "conv_weight")
+    for i in range(TILES):
+        bias[i : i + 1, :] = conv_bias[i * ROWS : (i + 1) * ROWS].reshape(1, ROWS)
 
     def convolve(i, carry):
         ext[i, 8:MSG, :] = conv_input[:, lanes(i)].astype(F32)
-        ext[i, 0:8, :] = rim[:, lanes(i)].astype(F32)[8:16]
-        pre = conv_bias[:, lanes(i)] + conv_weight[TAPS - 1 : TAPS, lanes(i)] * ext[i, 8:MSG, :]
+        ext[i, 0:8, :] = jnp.zeros((8, ROWS), F32)
+        pre = bias[pl.ds(i, 1), :] + conv_weight[TAPS - 1 : TAPS, lanes(i)] * ext[i, 8:MSG, :]
         for o in range(1, TAPS):
             tap = conv_weight[TAPS - 1 - o : TAPS - o, lanes(i)]
             pre = pre + tap * ext[i, 8 - o : MSG - o, :] * same_before[o - 1]
@@ -267,6 +316,35 @@
         return carry
 
     lax.fori_loop(0, TILES, convolve, 0)
+
+    arrived("gate_input", "reference_out", "norm_gain")
+
+    def gates(j, carry):
+        gate = gate_input[:, lanes(j)].astype(F32)
+        sigma = sigmoid(gate)
+        gate_act[j] = gate * sigma
+        gate_slope[j] = sigma * (1.0 + gate * (1.0 - sigma))
+        for half in range(2):
+            across = tall(row_of(LOG, 2 * j + half))
+            gap = across.T - across
+            decay[2 * j + half] = jnp.exp(jnp.where(mask[...] > 0.0, gap, -1e30))
+        return carry
+
+    lax.fori_loop(0, PAIRS, gates, 0)
+    rim_copy.wait_recv()
+
+    def convolve_top(i, carry):
+        ext[i, 0:8, :] = rim[:, lanes(i)].astype(F32)[8:16]
+        pre = bias[pl.ds(i, 1), :] + conv_weight[TAPS - 1 : TAPS, lanes(i)] * ext[i, 8:16, :]
+        for o in range(1, TAPS):
+            tap = conv_weight[TAPS - 1 - o : TAPS - o, lanes(i)]
+            pre = pre + tap * ext[i, 8 - o : 16 - o, :] * same_before[o - 1][0:8]
+        sigma = sigmoid(pre)
+        act[i, 0:8, :] = pre * sigma
+        slope[i, 0:8, :] = sigma * (1.0 + pre * (1.0 - sigma))
+        return carry
+
+    lax.fori_loop(0, TILES, convolve_top, 0)
 
     b_rows = act[PAIRS]
     c_rows = act[PAIRS + 1]
@@ -280,7 +358,7 @@
     def local_state(j, carry):
         part = act[j] * w_out_x[j]
         weighted[j] = part
-        msg_f[j, 0:ROWS, :] = product((bc[4], bc[5]), split(part))
+        msg_f[j, HEAD:MSG, :] = product((bc[4], bc[5]), split(part))
         return carry
 
     theirs = (1 - core) * CHIPS
@@ -291,132 +369,197 @@
         parts = []
         for half in range(2):
             h = 2 * j + half
-            across = tall(row_of(LOG, h))
-            gap = across.T - across
-            matrix = jnp.exp(jnp.where(mask[...] > 0.0, gap, -1e30))
-            decay[h] = matrix
-            mixed = scores[...] * matrix * row_of(STEP, h)
+            mixed = scores[...] * decay[h] * row_of(STEP, h)
             mix[h] = mixed
             parts.append(product(split(mixed), x_pair))
         inner[j] = jnp.where(first_half, parts[0], parts[1])
-        gate = gate_input[:, lanes(j)].astype(F32)
-        sigma = sigmoid(gate)
-        gate_act[j] = gate * sigma
-        gate_slope[j] = sigma * (1.0 + gate * (1.0 - sigma))
         return carry
 
     def scan(buffers, base, reverse, fill, work, result):
-        msg, near, chip, row, zin, zout, back, own, other = buffers
-        lax.fori_loop(theirs, theirs + CHIPS, fill, 0)
-        near_copy = copy(msg.at[pl.ds(theirs, CHIPS)], near, base, (partner, tp))
-        near_copy.start()
+        msg, near, chip, row, zin, zout, zfar, back, own, other = buffers
+        is_first = core == (1 if reverse else 0)
+        rank = 3 - zpos if reverse else zpos
+
+        def ranked(place):
+            return (chip_at(3 - place if reverse else place, xpos), tp)
+
+        up = ranked(jnp.minimum(rank + 1, 3))
+        far = ranked(jnp.where(rank == 0, 3, 2))
+        one = jnp.ones((1, ROWS), F32)
+        zero = jnp.zeros((1, ROWS), F32)
+
+        @pl.when(rank == 0)
+        def _():
+            zin[...] = jnp.zeros((MSG, ROWS), F32)
+
+        @pl.when(rank <= 1)
+        def _():
+            zfar[...] = jnp.zeros((ROWS, ROWS), F32)
+
+        near_copies = []
+        for q in range(CHIPS):
+            fill(theirs + q, 0)
+            near_copies.append(copy(msg.at[theirs + q], near.at[q], base + q, (partner, tp)))
+            near_copies[-1].start()
         lax.fori_loop(mine, mine + CHIPS, fill, 0)
-        near_copy.wait_recv()
-        is_first = core == (1 if reverse else 0)
-
-        def combine(q, carry):
-            my_pass = msg[mine + q, ROWS : ROWS + 1, :]
-            their_pass = near[q, ROWS : ROWS + 1, :]
+        for q in range(CHIPS):
+            near_copies[q].wait_recv()
+            my_pass = msg[mine + q, 0:1, :]
+            their_pass = near[q, 0:1, :]
             my_scale = jnp.where(is_first, their_pass, 1.0)
             their_scale = jnp.where(is_first, 1.0, my_pass)
-            chip[q, 0:ROWS, :] = (
-                msg[mine + q, 0:ROWS, :] * my_scale + near[q, 0:ROWS, :] * their_scale
+            chip[q, HEAD:MSG, :] = (
+                msg[mine + q, HEAD:MSG, :] * my_scale + near[q, HEAD:MSG, :] * their_scale
             )
-            chip[q, ROWS:MSG, :] = jnp.broadcast_to(my_pass * their_pass, (8, ROWS))
-            return carry
-
-        lax.fori_loop(0, CHIPS, combine, 0)
+            chip[q, 0:HEAD, :] = jnp.broadcast_to(my_pass * their_pass, (HEAD, ROWS))
+
+        def place(k):
+            return slice(0 if k == 0 else HEAD + k * PIECE, HEAD + (k + 1) * PIECE)
+
+        def piece(k):
+            return slice(k * PIECE, (k + 1) * PIECE)
+
+        def body(k):
+            return slice(HEAD + k * PIECE, HEAD + (k + 1) * PIECE)
+
         across = []
-        for step in range(1, CHIPS):
-            there = lax.rem(xpos + step, CHIPS)
-            across.append(
-                copy(chip.at[there], row.at[xpos], base + step, (chip_at(zpos, there), tp))
-            )
-            across[-1].start()
+        for k in range(CHUNKS):
+            sem = base + CHIPS + k * 3
+            for step in range(1, CHIPS):
+                there = lax.rem(xpos + step, CHIPS)
+                across.append(
+                    copy(
+                        chip.at[there, place(k)],
+                        row.at[xpos, place(k)],
+                        sem + step - 1,
+                        (chip_at(zpos, there), tp),
+                    )
+                )
+                across[-1].start()
         row[xpos] = chip[xpos]
-        for each in across:
-            each.wait_recv()
+        lax.fori_loop(0, SOON, work, 0)
         order = list(range(CHIPS))
         if reverse:
             order = order[::-1]
-        order_pass = jnp.ones((1, ROWS), F32)
-        running = None
-        back_scale = []
-        for place, x in enumerate(order):
-            back_scale.append(order_pass)
-            here_pass = row[x, ROWS : ROWS + 1, :]
-            if place == 0:
-                running = row[x, 0:ROWS, :]
-            else:
-                back[x] = running
-                running = running * here_pass + row[x, 0:ROWS, :]
-            order_pass = order_pass * here_pass
-        zout[...] = running
-        at_start = zpos == (3 if reverse else 0)
-        at_end = zpos == (0 if reverse else 3)
-        rank = 3 - zpos if reverse else zpos
-        early = (rank * PAIRS) // 3
-        up = chip_at(jnp.maximum(zpos - 1, 0) if reverse else jnp.minimum(zpos + 1, 3), xpos)
-        lax.fori_loop(0, early, work, 0)
-
-        @pl.when(jnp.logical_not(at_start))
-        def _():
-            copy(zout, zin, base + 4, (up, tp)).wait_recv()
-            zout[...] = zout[...] + zin[...] * order_pass
-
-        @pl.when(at_start)
-        def _():
-            zin[...] = jnp.zeros((ROWS, ROWS), F32)
-
-        @pl.when(jnp.logical_not(at_end))
-        def _():
-            copy(zout, zin, base + 4, (up, tp)).start()
-
-        for place, x in enumerate(order):
-            if place == 0:
-                back[x] = zin[...]
-            else:
-                back[x] = back[x] + zin[...] * back_scale[place]
+        early = SOON + jnp.where(rank == 0, 0, EARLY)
+        chain = base + CHIPS + 3 * CHUNKS
+        around = chain + CHUNKS
+        home = around + CHUNKS
+
+        def step_up(k):
+            return copy(zout.at[place(k)], zin.at[place(k)], chain + k, up)
+
+        def step_far(k, src):
+            return copy(src, zfar.at[piece(k)], around + k, far)
+
+        held = []
         returned = []
-        for step in range(1, CHIPS):
-            there = lax.rem(xpos + step, CHIPS)
-            returned.append(
-                copy(back.at[there], own.at[xpos], base + 4 + step, (chip_at(zpos, there), tp))
-            )
-            returned[-1].start()
+        for k in range(CHUNKS):
+            for each in across[3 * k : 3 * k + 3]:
+                each.wait_recv()
+            if k == 0:
+                passes = [row[x, 0:1, :] for x in order]
+                scales = [one]
+                for x_pass in passes:
+                    scales.append(scales[-1] * x_pass)
+            running = row[order[0], body(k), :]
+            entering = [None]
+            for x, x_pass in zip(order[1:], passes[1:]):
+                entering.append(running)
+                running = running * x_pass + row[x, body(k), :]
+            held.append(entering)
+            zout[body(k), :] = running
+            if k == 0:
+                zout[0:HEAD, :] = jnp.broadcast_to(scales[CHIPS], (HEAD, ROWS))
+
+            @pl.when(rank == 2)
+            def _():
+                step_up(k).wait_recv()
+                if k == 0:
+                    zout[0:HEAD, :] = zout[0:HEAD, :] * zin[0:HEAD, :]
+                zout[body(k), :] = zout[body(k), :] + zin[body(k), :] * scales[CHIPS]
+
+            @pl.when(rank <= 2)
+            def _():
+                step_up(k).start()
+
+            @pl.when(rank == 0)
+            def _():
+                step_far(k, zout.at[body(k)]).start()
+
+            @pl.when(rank == 3)
+            def _():
+                step_far(k, zfar.at[piece(k)]).wait_recv()
+                step_far(k, zfar.at[piece(k)]).start()
+
+        lax.fori_loop(SOON, early, work, 0)
+        for k in range(CHUNKS):
+
+            @pl.when(rank == 2)
+            def _():
+                step_far(k, zfar.at[piece(k)]).wait_recv()
+
+            @pl.when((rank == 1) | (rank == 3))
+            def _():
+                step_up(k).wait_recv()
+
+            from_before = zin[body(k), :] + zfar[piece(k), :] * zin[0:1, :]
+            for x, reached, scale in zip(order, held[k], scales):
+                back[x, piece(k), :] = (
+                    from_before if reached is None else reached + from_before * scale
+                )
+            for step in range(1, CHIPS):
+                there = lax.rem(xpos + step, CHIPS)
+                returned.append(
+                    copy(
+                        back.at[there, piece(k)],
+                        own.at[xpos, piece(k)],
+                        home + k * 3 + step - 1,
+                        (chip_at(zpos, there), tp),
+                    )
+                )
+                returned[-1].start()
         own[xpos] = back[xpos]
         lax.fori_loop(early, PAIRS, work, 0)
-        for each in returned:
+        last = []
+        for k in range(CHUNKS):
+            for each in returned[3 * k : 3 * k + 3]:
+                each.wait_recv()
+            for q in range(CHIPS):
+                my_pass = msg[mine + q, 0:1, :]
+                their_pass = near[q, 0:1, :]
+                coming = own[q, piece(k), :]
+                other[q, piece(k), :] = coming * jnp.where(is_first, my_pass, one) + msg[
+                    mine + q, body(k), :
+                ] * jnp.where(is_first, one, zero)
+                result[mine + q, piece(k), :] = coming * jnp.where(
+                    is_first, one, their_pass
+                ) + near[q, body(k), :] * jnp.where(is_first, zero, one)
+            last.append(
+                copy(
+                    other.at[:, piece(k)],
+                    result.at[pl.ds(mine, CHIPS), piece(k)],
+                    home + 3 * CHUNKS + k,
+                    (partner, tp),
+                )
+            )
+            last[-1].start()
+        for each in last:
             each.wait_recv()
 
-        def spread(q, carry):
-            my_pass = msg[mine + q, ROWS : ROWS + 1, :]
-            their_pass = near[q, ROWS : ROWS + 1, :]
-            entering = own[q]
-            one = jnp.ones((1, ROWS), F32)
-            zero = jnp.zeros((1, ROWS), F32)
-            other[q] = entering * jnp.where(is_first, my_pass, one) + msg[
-                mine + q, 0:ROWS, :
-            ] * jnp.where(is_first, one, zero)
-            result[mine + q] = entering * jnp.where(is_first, one, their_pass) + near[
-                q, 0:ROWS, :
-            ] * jnp.where(is_first, zero, one)
-            return carry
-
-        lax.fori_loop(0, CHIPS, spread, 0)
-        last = copy(other, result.at[pl.ds(mine, CHIPS)], base + 8, (partner, tp))
-        last.start()
-        last.wait_recv()
-
         def drain():
-            near_copy.wait_send()
-            for each in across + returned:
+            for each in near_copies + across + returned + last:
                 each.wait_send()
-            last.wait_send()
-
-            @pl.when(jnp.logical_not(at_end))
+
+            @pl.when(rank <= 2)
             def _():
-                copy(zout, zin, base + 4, (up, tp)).wait_send()
+                for k in range(CHUNKS):
+                    step_up(k).wait_send()
+
+            @pl.when((rank == 0) | (rank == 3))
+            def _():
+                for k in range(CHUNKS):
+                    step_far(k, zfar.at[piece(k)]).wait_send()
 
         return drain
 
@@ -424,8 +567,8 @@
         return local_state(j, carry)
 
     scores[...] = product((c_high, c_low), (b_high, b_low), (1, 1))
-    forward = (msg_f, near_f, chip_f, row_f, zin_f, zout_f, back_f, own_f, other_f)
-    drain_forward = scan(forward, 1, False, fill_forward, within, carried)
+    forward = (msg_f, near_f, chip_f, row_f, zin_f, zout_f, zfar_f, back_f, own_f, other_f)
+    drain_forward = scan(forward, 9, False, fill_forward, within, carried)
 
     sums[...] = jnp.zeros((4, ROWS, ROWS), F32)
 
@@ -462,7 +605,7 @@
     tp_copies = []
     for step in range(1, NTP):
         there = lax.rem(tp + step, NTP)
-        tp_copies.append(copy(totals.at[tp], totals.at[tp], 18 + step, (ctx, there)))
+        tp_copies.append(copy(totals.at[tp], totals.at[tp], 1 + step, (ctx, there)))
         tp_copies[-1].start()
     for each in tp_copies:
         each.wait_recv()
@@ -496,7 +639,7 @@
         grad_y[j] = into
         entering = into * w_in_x[j]
         grad_in[j] = entering
-        msg_b[j, 0:ROWS, :] = product((bc[6], bc[7]), split(entering))
+        msg_b[j, HEAD:MSG, :] = product((bc[6], bc[7]), split(entering))
         return carry
 
     grad_scores[...] = jnp.zeros((ROWS, ROWS), F32)
@@ -533,8 +676,8 @@
         grad_c[...] = grad_c[...] + product(split(grad_in[j]), split(carried[j]), (1, 1))
         return carry
 
-    backward = (msg_b, near_b, chip_b, row_b, zin_b, zout_b, back_b, own_b, other_b)
-    drain_backward = scan(backward, 10, True, fill_backward, within_back, adjoint)
+    backward = (msg_b, near_b, chip_b, row_b, zin_b, zout_b, zfar_b, back_b, own_b, other_b)
+    drain_backward = scan(backward, 9 + SCAN_SEMS, True, fill_backward, within_back, adjoint)
 
     def finish(j, carry):
         coming = adjoint[j]
@@ -560,9 +703,8 @@
     grad_pre[PAIRS + 1, 0:ROWS, :] = by_c * slope[PAIRS + 1]
     rim_out[PAIRS] = grad_pre[PAIRS, 0:8, :]
     rim_out[PAIRS + 1] = grad_pre[PAIRS + 1, 0:8, :]
-    rim_back = copy(rim_out, rim_in, 26, (before, tp))
+    rim_back = copy(rim_out, rim_in, 1, (before, tp))
     rim_back.start()
-
     grad_weight = table[GWEIGHT]
     leaving = grad_weight * table[WOUT]
     at_end = jnp.sum(leaving, axis=1, keepdims=True) + jnp.sum(
@@ -621,15 +763,31 @@
         pltpu.VMEM((CHIPS, MSG, ROWS), F32),
         pltpu.VMEM((CHIPS, MSG, ROWS), F32),
         pltpu.VMEM((CHIPS, MSG, ROWS), F32),
-        one,
+        pltpu.VMEM((MSG, ROWS), F32),
+        pltpu.VMEM((MSG, ROWS), F32),
         one,
         pltpu.VMEM((CHIPS, *square), F32),
         pltpu.VMEM((CHIPS, *square), F32),
         pltpu.VMEM((CHIPS, *square), F32),
     ]
     vmem = pl.BlockSpec(memory_space=pltpu.VMEM)
-    smem = pl.BlockSpec(memory_space=pltpu.SMEM)
+    far = pl.BlockSpec(memory_space=pltpu.HBM)
+    held = [
+        pltpu.SMEM((2,), jnp.int32),
+        pltpu.SMEM((DOCS,), jnp.int32),
+        pltpu.VMEM((ROWS, TILES * ROWS), BF16),
+        pltpu.VMEM((ROWS, GROUP_WIDTH), BF16),
+        pltpu.VMEM((16, ROWS), F32),
+        pltpu.VMEM((TAPS, TILES * ROWS), F32),
+        pltpu.VMEM((TILES * ROWS,), F32),
+        pltpu.VMEM((1, 16), F32),
+        pltpu.VMEM((1, 16), F32),
+        pltpu.VMEM((1, GROUP_WIDTH), F32),
+        pltpu.VMEM((ROWS, GROUP_WIDTH), BF16),
+    ]
     scratch = [
+        *held,
+        pltpu.VMEM((TILES, ROWS), F32),
         pltpu.VMEM((16, TILES * ROWS), BF16),
         padded,
         by_tile,
@@ -654,6 +812,7 @@
         one,
         one,
         pltpu.VMEM((8, *square), BF16),
+        pltpu.VMEM((2, PAIRS, *square), BF16),
         one,
         one,
         one,
@@ -662,8 +821,9 @@
         pltpu.VMEM((NTP, 8, ROWS), F32),
         *scans,
         *scans,
-        pltpu.SemaphoreType.DMA((27,)),
-        pltpu.SemaphoreType.DMA((27,)),
+        pltpu.SemaphoreType.DMA((9 + 2 * SCAN_SEMS,)),
+        pltpu.SemaphoreType.DMA((9 + 2 * SCAN_SEMS,)),
+        pltpu.SemaphoreType.DMA((11,)),
     ]
     return pl.pallas_call(
         kernel,
@@ -672,24 +832,24 @@
             jax.ShapeDtypeStruct(gate_input.shape, BF16),
             jax.ShapeDtypeStruct(dt_raw.shape, F32),
         ),
-        in_specs=[smem] * 2 + [vmem] * 9,
+        in_specs=[far] * 11,
         out_specs=(vmem, vmem, vmem),
         scratch_shapes=scratch,
         compiler_params=pltpu.CompilerParams(
-            collective_id=0, has_side_effects=True, vmem_limit_bytes=60 * 1024 * 1024
+            collective_id=0, has_side_effects=True, vmem_limit_bytes=48 * 1024 * 1024
         ),
     )(
-        labels,
-        doc_lengths,
-        conv_input,
-        gate_input,
-        dt_raw,
-        conv_weight,
-        conv_bias.reshape(1, -1),
-        dt_bias.reshape(1, -1),
-        a_log.reshape(1, -1),
-        norm_gain.reshape(1, -1),
-        reference_out,
+        pltpu.with_memory_space_constraint(labels, pltpu.HBM),
+        pltpu.with_memory_space_constraint(doc_lengths, pltpu.HBM),
+        pltpu.with_memory_space_constraint(conv_input, pltpu.HBM),
+        pltpu.with_memory_space_constraint(gate_input, pltpu.HBM),
+        pltpu.with_memory_space_constraint(dt_raw, pltpu.HBM),
+        pltpu.with_memory_space_constraint(conv_weight, pltpu.HBM),
+        pltpu.with_memory_space_constraint(conv_bias, pltpu.HBM),
+        pltpu.with_memory_space_constraint(dt_bias.reshape(1, -1), pltpu.HBM),
+        pltpu.with_memory_space_constraint(a_log.reshape(1, -1), pltpu.HBM),
+        pltpu.with_memory_space_constraint(norm_gain.reshape(1, -1), pltpu.HBM),
+        pltpu.with_memory_space_constraint(reference_out, pltpu.HBM),
     )
 
 

time: 85.1 us -> 66.7 us (0.78)
  Pallas kernels: 79.9 us -> 63.9 us
  local copies, waits for them, and re-layouts: 4.36 us -> 2.03 us
    pallas_call x1, Pallas kernels: 79.9 us -> 63.9 us  [on_device(): pl.pallas_call(kernel, out_shape=(jax.ShapeDtypeStruct(conv_input.shape,...]
    reshape x1 -> x0, local copies, waits for them, and re-layouts: 1.29 us -> none  [on_device(): conv_bias.reshape(1, -1)]
    unnamed x7 -> x3, local copies, waits for them, and re-layouts: 3.07 us -> 2.03 us
where the time goes in v2:
time: 66.7 us; the launch traced here: 66.6 us
  Pallas kernels  63.9 us (96%)
  local copies, waits for them, and re-layouts  2.03 us (3%)
    pallas_call x1, Pallas kernels, on_device(): pl.pallas_call(kernel, out_shape=(jax.ShapeDtypeStruct(conv_input.shape,...  63.9 us
    unnamed x3, local copies, waits for them, and re-layouts  2.03 us

profile of v2, /device:TPU:1, one launch (start us, length us, event | category | flops | bytes accessed | tf_op | source)
XLA Modules:
  0.0 66.6 jit_solution(15547269646415010805)
XLA Ops:
  0.6 63.9 %shard_map.130 = (bf16[128,1280]{1,0:T(8,128)(2,1)S(1)}, bf16[128,1024]{1,0:T(8,128)(2,1)S(1)}, f32[16,128]{1,0:T(8,128)S(1)}) custom-call(s32[2]{0:T(128)} %labels_hbm.1, s32[8]{0:T(128)} %doc_lengths_hbm.1, bf16[128,1280]{1,0:T(8,128)(2,1)} %conv_input_hbm.1, bf16[128,1024]{1,0:T(8,128)(2,1)} %gate_input_hbm.1, f32[16,128]{1,0:T(8,128)} %dt_raw_hbm.1, ...), custom_call_target="tpu_custom_call" | custom-call | tf_op jit(solution)/shard_map/pallas_call | solution.py:828
  64.5 0.7 %copy.17 = bf16[128,1280]{1,0:T(8,128)(2,1)} copy(bf16[128,1280]{1,0:T(8,128)(2,1)S(1)} %get-tuple-element.6) | data formatting | bytes 655360
  65.3 0.7 %copy.18 = bf16[128,1024]{1,0:T(8,128)(2,1)} copy(bf16[128,1024]{1,0:T(8,128)(2,1)S(1)} %get-tuple-element.7) | data formatting | bytes 524288
  66.0 0.6 copy.19

commit v3 on v2

--- a/solution.py
+++ b/solution.py
@@ -290,7 +290,7 @@
         msg_b[j, 0:HEAD, :] = pass_rows
         return carry
 
-    lax.fori_loop(0, PAIRS, expand, 0)
+    lax.fori_loop(0, PAIRS, expand, 0, unroll=8)
 
     same_before = [
         jnp.where(doc_of(first_pos + row_index - o) == docs_down, 1.0, 0.0) for o in range(1, TAPS)
@@ -315,7 +315,7 @@
         slope[i] = sigma * (1.0 + pre * (1.0 - sigma))
         return carry
 
-    lax.fori_loop(0, TILES, convolve, 0)
+    lax.fori_loop(0, TILES, convolve, 0, unroll=10)
 
     arrived("gate_input", "reference_out", "norm_gain")
 
@@ -330,7 +330,7 @@
             decay[2 * j + half] = jnp.exp(jnp.where(mask[...] > 0.0, gap, -1e30))
         return carry
 
-    lax.fori_loop(0, PAIRS, gates, 0)
+    lax.fori_loop(0, PAIRS, gates, 0, unroll=8)
     rim_copy.wait_recv()
 
     def convolve_top(i, carry):
@@ -344,7 +344,7 @@
         slope[i, 0:8, :] = sigma * (1.0 + pre * (1.0 - sigma))
         return carry
 
-    lax.fori_loop(0, TILES, convolve_top, 0)
+    lax.fori_loop(0, TILES, convolve_top, 0, unroll=10)
 
     b_rows = act[PAIRS]
     c_rows = act[PAIRS + 1]
@@ -401,7 +401,8 @@
             fill(theirs + q, 0)
             near_copies.append(copy(msg.at[theirs + q], near.at[q], base + q, (partner, tp)))
             near_copies[-1].start()
-        lax.fori_loop(mine, mine + CHIPS, fill, 0)
+        for q in range(CHIPS):
+            fill(mine + q, 0)
         for q in range(CHIPS):
             near_copies[q].wait_recv()
             my_pass = msg[mine + q, 0:1, :]
@@ -425,7 +426,7 @@
         across = []
         for k in range(CHUNKS):
             sem = base + CHIPS + k * 3
-            for step in range(1, CHIPS):
+            for step in (2, 1, 3):
                 there = lax.rem(xpos + step, CHIPS)
                 across.append(
                     copy(
@@ -508,7 +509,7 @@
                 back[x, piece(k), :] = (
                     from_before if reached is None else reached + from_before * scale
                 )
-            for step in range(1, CHIPS):
+            for step in (2, 1, 3):
                 there = lax.rem(xpos + step, CHIPS)
                 returned.append(
                     copy(
@@ -586,7 +587,7 @@
         sums[3] = sums[3] + target * target
         return carry
 
-    lax.fori_loop(0, PAIRS, outputs, 0)
+    lax.fori_loop(0, PAIRS, outputs, 0, unroll=8)
     square = jnp.sum(sums[0].T, axis=0, keepdims=True) / GROUP_WIDTH + 1e-05
     dot_here = jnp.sum(sums[1].T, axis=0, keepdims=True)
     self_here = jnp.sum(sums[2].T, axis=0, keepdims=True)
@@ -695,7 +696,7 @@
         grad_b[...] = grad_b[...] + product(split(weighted[j]), coming_pair, (1, 1))
         return carry
 
-    lax.fori_loop(0, PAIRS, finish, 0)
+    lax.fori_loop(0, PAIRS, finish, 0, unroll=8)
     via_scores = grad_scores[...]
     by_b = grad_b[...] + product(split(via_scores.T), (bc[2], bc[3]))
     by_c = grad_c[...] + product(split(via_scores), (bc[0], bc[1]))
@@ -735,7 +736,7 @@
         out_input[:, lanes(i)] = total.astype(BF16)
         return carry
 
-    lax.fori_loop(0, TILES, spread_taps, 0)
+    lax.fori_loop(0, TILES, spread_taps, 0, unroll=10)
     drain_backward()
     rim_back.wait_send()
 

time: 66.7 us -> 62.9 us (0.943)
  Pallas kernels: 63.9 us -> 60.2 us
    pallas_call x1, Pallas kernels: 63.9 us -> 60.2 us  [on_device(): pl.pallas_call(kernel, out_shape=(jax.ShapeDtypeStruct(conv_input.shape,...]
where the time goes in v3:
time: 62.9 us; the launch traced here: 62.8 us
  Pallas kernels  60.2 us (96%)
  local copies, waits for them, and re-layouts  2.03 us (3%)
  between operations  0.64 us (1%)
    pallas_call x1, Pallas kernels, on_device(): pl.pallas_call(kernel, out_shape=(jax.ShapeDtypeStruct(conv_input.shape,...  60.2 us
    unnamed x3, local copies, waits for them, and re-layouts  2.03 us

profile of v3, /device:TPU:1, one launch (start us, length us, event | category | flops | bytes accessed | tf_op | source)
XLA Modules:
  0.0 62.8 jit_solution(14647238030481256345)
XLA Ops:
  0.6 60.2 %shard_map.130 = (bf16[128,1280]{1,0:T(8,128)(2,1)S(1)}, bf16[128,1024]{1,0:T(8,128)(2,1)S(1)}, f32[16,128]{1,0:T(8,128)S(1)}) custom-call(s32[2]{0:T(128)} %labels_hbm.1, s32[8]{0:T(128)} %doc_lengths_hbm.1, bf16[128,1280]{1,0:T(8,128)(2,1)} %conv_input_hbm.1, bf16[128,1024]{1,0:T(8,128)(2,1)} %gate_input_hbm.1, f32[16,128]{1,0:T(8,128)} %dt_raw_hbm.1, ...), custom_call_target="tpu_custom_call" | custom-call | tf_op jit(solution)/shard_map/pallas_call | solution.py:829
  60.8 0.7 %copy.17 = bf16[128,1280]{1,0:T(8,128)(2,1)} copy(bf16[128,1280]{1,0:T(8,128)(2,1)S(1)} %get-tuple-element.6) | data formatting | bytes 655360
  61.5 0.7 %copy.18 = bf16[128,1024]{1,0:T(8,128)(2,1)} copy(bf16[128,1024]{1,0:T(8,128)(2,1)S(1)} %get-tuple-element.7) | data formatting | bytes 524288
  62.2 0.6 copy.19

commit v4 on v3

--- a/solution.py
+++ b/solution.py
@@ -375,7 +375,7 @@
         inner[j] = jnp.where(first_half, parts[0], parts[1])
         return carry
 
-    def scan(buffers, base, reverse, fill, work, result):
+    def scan(buffers, base, reverse, fill, work, afterwards, result):
         msg, near, chip, row, zin, zout, zfar, back, own, other = buffers
         is_first = core == (1 if reverse else 0)
         rank = 3 - zpos if reverse else zpos
@@ -522,6 +522,7 @@
                 returned[-1].start()
         own[xpos] = back[xpos]
         lax.fori_loop(early, PAIRS, work, 0)
+        afterwards()
         last = []
         for k in range(CHUNKS):
             for each in returned[3 * k : 3 * k + 3]:
@@ -569,7 +570,7 @@
 
     scores[...] = product((c_high, c_low), (b_high, b_low), (1, 1))
     forward = (msg_f, near_f, chip_f, row_f, zin_f, zout_f, zfar_f, back_f, own_f, other_f)
-    drain_forward = scan(forward, 9, False, fill_forward, within, carried)
+    drain_forward = scan(forward, 9, False, fill_forward, within, lambda: None, carried)
 
     sums[...] = jnp.zeros((4, ROWS, ROWS), F32)
 
@@ -678,7 +679,16 @@
         return carry
 
     backward = (msg_b, near_b, chip_b, row_b, zin_b, zout_b, zfar_b, back_b, own_b, other_b)
-    drain_backward = scan(backward, 9 + SCAN_SEMS, True, fill_backward, within_back, adjoint)
+    def close_scores():
+        via_scores = grad_scores[...]
+        grad_b[...] = product(split(via_scores.T), (bc[2], bc[3]))
+        by_c = grad_c[...] + product(split(via_scores), (bc[0], bc[1]))
+        grad_pre[PAIRS + 1, 0:ROWS, :] = by_c * slope[PAIRS + 1]
+        rim_out[PAIRS + 1] = grad_pre[PAIRS + 1, 0:8, :]
+
+    drain_backward = scan(
+        backward, 9 + SCAN_SEMS, True, fill_backward, within_back, close_scores, adjoint
+    )
 
     def finish(j, carry):
         coming = adjoint[j]
@@ -687,25 +697,26 @@
         grad = grad_x[j] + later * w_out_x[j]
         grad_pre[j, 0:ROWS, :] = grad * slope[j]
         rim_out[j] = grad_pre[j, 0:8, :]
-        by_weight = halves(later * act[j])
+        read[j] = later * act[j]
+        grad_b[...] = grad_b[...] + product(split(weighted[j]), coming_pair, (1, 1))
+        return carry
+
+    lax.fori_loop(0, PAIRS, finish, 0, unroll=8)
+    grad_pre[PAIRS, 0:ROWS, :] = grad_b[...] * slope[PAIRS]
+    rim_out[PAIRS] = grad_pre[PAIRS, 0:8, :]
+    rim_back = copy(rim_out, rim_in, 1, (before, tp))
+    rim_back.start()
+
+    def finish_rows(j, carry):
+        by_weight = halves(read[j])
         table[GWEIGHT, pl.ds(2 * j, 1), :] = by_weight[0]
         table[GWEIGHT, pl.ds(2 * j + 1, 1), :] = by_weight[1]
-        ended = jnp.sum(carried[j] * coming, axis=0, keepdims=True)
+        ended = jnp.sum(carried[j] * adjoint[j], axis=0, keepdims=True)
         table[GEND, pl.ds(2 * j, 1), :] = jnp.where(lane_row < 64, ended, 0.0)
         table[GEND, pl.ds(2 * j + 1, 1), :] = jnp.where(lane_row < 64, 0.0, ended)
-        grad_b[...] = grad_b[...] + product(split(weighted[j]), coming_pair, (1, 1))
-        return carry
-
-    lax.fori_loop(0, PAIRS, finish, 0, unroll=8)
-    via_scores = grad_scores[...]
-    by_b = grad_b[...] + product(split(via_scores.T), (bc[2], bc[3]))
-    by_c = grad_c[...] + product(split(via_scores), (bc[0], bc[1]))
-    grad_pre[PAIRS, 0:ROWS, :] = by_b * slope[PAIRS]
-    grad_pre[PAIRS + 1, 0:ROWS, :] = by_c * slope[PAIRS + 1]
-    rim_out[PAIRS] = grad_pre[PAIRS, 0:8, :]
-    rim_out[PAIRS + 1] = grad_pre[PAIRS + 1, 0:8, :]
-    rim_back = copy(rim_out, rim_in, 1, (before, tp))
-    rim_back.start()
+        return carry
+
+    lax.fori_loop(0, PAIRS, finish_rows, 0, unroll=8)
     grad_weight = table[GWEIGHT]
     leaving = grad_weight * table[WOUT]
     at_end = jnp.sum(leaving, axis=1, keepdims=True) + jnp.sum(
@@ -826,7 +837,7 @@
         pltpu.SemaphoreType.DMA((9 + 2 * SCAN_SEMS,)),
         pltpu.SemaphoreType.DMA((11,)),
     ]
-    return pl.pallas_call(
+    results = pl.pallas_call(
         kernel,
         out_shape=(
             jax.ShapeDtypeStruct(conv_input.shape, BF16),
@@ -852,6 +863,27 @@
         pltpu.with_memory_space_constraint(norm_gain.reshape(1, -1), pltpu.HBM),
         pltpu.with_memory_space_constraint(reference_out, pltpu.HBM),
     )
+    return pl.pallas_call(
+        put_out,
+        out_shape=tuple(jax.ShapeDtypeStruct(each.shape, each.dtype) for each in results),
+        in_specs=[vmem] * 3,
+        out_specs=(far,) * 3,
+        scratch_shapes=[pltpu.SemaphoreType.DMA((3,))],
+        compiler_params=pltpu.CompilerParams(vmem_limit_bytes=8 * 1024 * 1024),
+    )(*results)
+
+
+def put_out(input_in, gate_in, dt_in, input_out, gate_out, dt_out, sem):
+    moves = [
+        pltpu.make_async_copy(src, dst, sem.at[place])
+        for place, (src, dst) in enumerate(
+            ((input_in, input_out), (gate_in, gate_out), (dt_in, dt_out))
+        )
+    ]
+    for move in moves:
+        move.start()
+    for move in moves:
+        move.wait()
 
 
 def solution(mesh):

time: 62.9 us -> 61.7 us (0.981)
  local copies, waits for them, and re-layouts: 2.03 us -> 0 us
  Pallas kernels: 60.2 us -> 61 us
    unnamed x3 -> x0, local copies, waits for them, and re-layouts: 2.03 us -> none
    pallas_call x0 -> x1, Pallas kernels: none -> 0.84 us  [on_device(): pl.pallas_call(put_out, out_shape=tuple((jax.ShapeDtypeStruct(each.shape,...]
where the time goes in v4:
time: 61.7 us; the launch traced here: 61.6 us
  Pallas kernels  61 us (99%)
  between operations  0.64 us (1%)
    pallas_call x1, Pallas kernels, on_device(): pl.pallas_call(kernel, out_shape=(jax.ShapeDtypeStruct(conv_input.shape,...  60.1 us

profile of v4, /device:TPU:1, one launch (start us, length us, event | category | flops | bytes accessed | tf_op | source)
XLA Modules:
  0.0 61.6 jit_solution(6460360677872848853)
XLA Ops:
  0.6 60.1 %shard_map.130 = (bf16[128,1280]{1,0:T(8,128)(2,1)S(1)}, bf16[128,1024]{1,0:T(8,128)(2,1)S(1)}, f32[16,128]{1,0:T(8,128)S(1)}) custom-call(s32[2]{0:T(128)} %labels_hbm.1, s32[8]{0:T(128)} %doc_lengths_hbm.1, bf16[128,1280]{1,0:T(8,128)(2,1)} %conv_input_hbm.1, bf16[128,1024]{1,0:T(8,128)(2,1)} %gate_input_hbm.1, f32[16,128]{1,0:T(8,128)} %dt_raw_hbm.1, ...), custom_call_target="tpu_custom_call" | custom-call | tf_op jit(solution)/shard_map/pallas_call | solution.py:840
  60.8 0.8 %shard_map.131 = (bf16[128,1280]{1,0:T(8,128)(2,1)}, bf16[128,1024]{1,0:T(8,128)(2,1)}, f32[16,128]{1,0:T(8,128)}) custom-call(bf16[128,1280]{1,0:T(8,128)(2,1)S(1)} %get-tuple-element.6.input_in, bf16[128,1024]{1,0:T(8,128)(2,1)S(1)} %get-tuple-element.7.gate_in, f32[16,128]{1,0:T(8,128)S(1)} %get-tuple-element.8.dt_in), custom_call_target="tpu_custom_call" | custom-call | tf_op jit(solution)/shard_map/pallas_call | solution.py:866

commit v5 on v4

--- a/solution.py
+++ b/solution.py
@@ -173,13 +173,14 @@
         return (z * CHIPS + x) * 2 + core
 
     barrier = pltpu.get_barrier_semaphore()
-    peers = [(partner, tp), (after, tp), (before, tp)]
-    for step in range(1, CHIPS):
-        peers.append((chip_at(zpos, lax.rem(xpos + step, CHIPS)), tp))
+    peers = [(after, tp), (before, tp)]
     peers.append((chip_at(lax.rem(zpos + 1, 4), xpos), tp))
     peers.append((chip_at(lax.rem(zpos + 3, 4), xpos), tp))
     for step in range(1, NTP):
         peers.append((ctx, lax.rem(tp + step, NTP)))
+    for step in range(1, CHIPS):
+        peers.append((chip_at(zpos, lax.rem(xpos + step, CHIPS)), tp))
+    peers.append((partner, tp))
     for peer in peers:
         pl.semaphore_signal(barrier, inc=1, device_id=peer, device_id_type=MESH)
 
@@ -319,7 +320,11 @@
 
     arrived("gate_input", "reference_out", "norm_gain")
 
+    sums[3] = jnp.zeros((ROWS, ROWS), F32)
+
     def gates(j, carry):
+        target = reference_out[:, lanes(j)].astype(F32)
+        sums[3] = sums[3] + target * target
         gate = gate_input[:, lanes(j)].astype(F32)
         sigma = sigmoid(gate)
         gate_act[j] = gate * sigma
@@ -570,9 +575,13 @@
 
     scores[...] = product((c_high, c_low), (b_high, b_low), (1, 1))
     forward = (msg_f, near_f, chip_f, row_f, zin_f, zout_f, zfar_f, back_f, own_f, other_f)
-    drain_forward = scan(forward, 9, False, fill_forward, within, lambda: None, carried)
-
-    sums[...] = jnp.zeros((4, ROWS, ROWS), F32)
+
+    def close_targets():
+        table[LOG, 0:1, :] = jnp.sum(sums[3].T, axis=0, keepdims=True)
+
+    drain_forward = scan(forward, 9, False, fill_forward, within, close_targets, carried)
+
+    sums[0:3] = jnp.zeros((3, ROWS, ROWS), F32)
 
     def outputs(j, carry):
         part = product((bc[2], bc[3]), split(carried[j])) * w_in_x[j]
@@ -585,21 +594,19 @@
         sums[0] = sums[0] + gated * gated
         sums[1] = sums[1] + gained * target
         sums[2] = sums[2] + gained * gained
-        sums[3] = sums[3] + target * target
         return carry
 
     lax.fori_loop(0, PAIRS, outputs, 0, unroll=8)
     square = jnp.sum(sums[0].T, axis=0, keepdims=True) / GROUP_WIDTH + 1e-05
     dot_here = jnp.sum(sums[1].T, axis=0, keepdims=True)
     self_here = jnp.sum(sums[2].T, axis=0, keepdims=True)
-    ref_here = jnp.sum(sums[3].T, axis=0, keepdims=True)
     inverse = lax.rsqrt(square)
     inverse = inverse * (1.5 - 0.5 * square * inverse * inverse)
     totals[tp] = jnp.concatenate(
         [
             dot_here * inverse,
             self_here * inverse * inverse,
-            ref_here,
+            table[LOG, 0:1, :],
             jnp.zeros((5, ROWS), F32),
         ],
         axis=0,

time: 61.7 us -> 61.7 us (level)
  no operation moved by 1% of the time
where the time goes in v5:
time: 61.7 us; the launch traced here: 61.6 us
  Pallas kernels  60.9 us (99%)
  between operations  0.64 us (1%)
    pallas_call x1, Pallas kernels, on_device(): pl.pallas_call(kernel, out_shape=(jax.ShapeDtypeStruct(conv_input.shape,...  60.1 us

profile of v5, /device:TPU:1, one launch (start us, length us, event | category | flops | bytes accessed | tf_op | source)
XLA Modules:
  0.0 61.6 jit_solution(18169192231088022588)
XLA Ops:
  0.6 60.1 %shard_map.130 = (bf16[128,1280]{1,0:T(8,128)(2,1)S(1)}, bf16[128,1024]{1,0:T(8,128)(2,1)S(1)}, f32[16,128]{1,0:T(8,128)S(1)}) custom-call(s32[2]{0:T(128)} %labels_hbm.1, s32[8]{0:T(128)} %doc_lengths_hbm.1, bf16[128,1280]{1,0:T(8,128)(2,1)} %conv_input_hbm.1, bf16[128,1024]{1,0:T(8,128)(2,1)} %gate_input_hbm.1, f32[16,128]{1,0:T(8,128)} %dt_raw_hbm.1, ...), custom_call_target="tpu_custom_call" | custom-call | tf_op jit(solution)/shard_map/pallas_call | solution.py:847
  60.7 0.8 %shard_map.131 = (bf16[128,1280]{1,0:T(8,128)(2,1)}, bf16[128,1024]{1,0:T(8,128)(2,1)}, f32[16,128]{1,0:T(8,128)}) custom-call(bf16[128,1280]{1,0:T(8,128)(2,1)S(1)} %get-tuple-element.6.input_in, bf16[128,1024]{1,0:T(8,128)(2,1)S(1)} %get-tuple-element.7.gate_in, f32[16,128]{1,0:T(8,128)S(1)} %get-tuple-element.8.dt_in), custom_call_target="tpu_custom_call" | custom-call | tf_op jit(solution)/shard_map/pallas_call | solution.py:873
